TPU v7x, 256 devices: a whole 4x4x8 slice. The times are simulated.
256 devices in a mesh: expert: 64 (over x, y, z_hi), hidden: 4 (over z_lo, core).
Axes of the slice: x: 4, y: 4, z: 8 (z_hi: 4, z_lo: 2; z = z_hi * 2 + z_lo), core: 2. Of those that a mesh axis runs over, the one named last changes fastest.
Arguments:
- tokens: bfloat16 [256, 196, 1024], P('expert'), may hold values from -32 to 32
- slot_keys: bfloat16 [1024, 128], replicated, may hold values from -1 to 1
- w_in: bfloat16 [128, 1024, 4096], P('expert', None, 'hidden'), may hold values from -0.1875 to 0.1875
- b_in: float32 [128, 4096], P('expert', 'hidden'), may hold values from -6 to 6
- w_out: bfloat16 [128, 4096, 1024], P('expert', 'hidden'), may hold values from -0.09375 to 0.09375
- b_out: float32 [128, 1024], replicated, may hold values from -6 to 6
- out_grad: bfloat16 [256, 196, 1024], P('expert'), may hold values from -6 to 6
Outputs:
- token_grad: bfloat16 [256, 196, 1024], P(('expert', 'hidden'))
All inputs are finite; a program needn't handle non-finite values.
Results may differ from a plain program's by a relative error of at most 0.028.
Values may be sent and summed in bfloat16 or wider, within the bound.
A program may use at most 64 MiB of HBM per device.

v0:
```python
import jax
import jax.numpy as jnp
from jax import lax
from jax.sharding import PartitionSpec as P


def gelu_slope(pre_act):
    return (
        0.5 * (1.0 + lax.erf(pre_act * 0.7071067811865476))
        + pre_act * jnp.exp(-0.5 * pre_act * pre_act) * 0.3989422804014327
    )


def send_home(term_fn, row_total, n_expert, quarter, local_experts, width, full_bias):
    n_hidden = lax.axis_size("hidden")
    term = term_fn(0, row_total).astype(jnp.bfloat16)
    term = term.reshape(n_hidden, n_expert, quarter, local_experts, width)
    moved = lax.all_to_all(term, "expert", split_axis=1, concat_axis=3, tiled=True)
    summed = lax.psum_scatter(
        moved.astype(jnp.float32).astype(jnp.bfloat16), "hidden", scatter_dimension=0, tiled=True
    ).astype(jnp.float32)
    summed = summed.reshape(quarter, n_expert * local_experts, width)
    return (summed + full_bias[None]).astype(jnp.bfloat16)


def local(tokens, slot_keys, w_in, b_in, w_out, b_out, out_grad):
    n_expert = lax.axis_size("expert")
    n_hidden = lax.axis_size("hidden")
    image_count, positions, width = tokens.shape
    quarter = image_count // n_hidden
    slot_count = slot_keys.shape[1]
    local_experts = w_in.shape[0]
    logits = jnp.einsum("btd,ds->bts", tokens, slot_keys, preferred_element_type=jnp.float32)
    dispatch = jax.nn.softmax(logits, axis=1).astype(jnp.bfloat16)
    combine = jax.nn.softmax(logits, axis=2).astype(jnp.bfloat16)
    slot_in = jnp.einsum(
        "bts,btd->bsd", dispatch, tokens, preferred_element_type=jnp.float32
    ).astype(jnp.bfloat16)
    slot_grad = jnp.einsum(
        "bts,btd->bsd", combine, out_grad, preferred_element_type=jnp.float32
    ).astype(jnp.bfloat16)
    grouped = (n_hidden, quarter, slot_count, width)
    sent_in, sent_grad = (
        lax.all_to_all(slot_in.reshape(grouped), "expert", split_axis=2, concat_axis=1, tiled=True),
        lax.all_to_all(
            slot_grad.reshape(grouped), "expert", split_axis=2, concat_axis=1, tiled=True
        ),
    )
    row_total = n_hidden * n_expert * quarter
    rows_in = sent_in.reshape(row_total, local_experts, width)
    rows_grad = sent_grad.reshape(row_total, local_experts, width)
    pre_act = (
        jnp.einsum("rkd,kdf->rkf", rows_in, w_in, preferred_element_type=jnp.float32) + b_in[None]
    )
    hidden_act = jax.nn.gelu(pre_act, approximate=False).astype(jnp.bfloat16)

    def output_term(row_start, row_count):
        return jnp.einsum("rkf,kfd->rkd", hidden_act, w_out, preferred_element_type=jnp.float32)

    slot_out = send_home(output_term, row_total, n_expert, quarter, local_experts, width, b_out)
    act_grad = jnp.einsum("rkd,kfd->rkf", rows_grad, w_out, preferred_element_type=jnp.float32)
    pre_grad = (act_grad * gelu_slope(pre_act)).astype(jnp.bfloat16)

    def input_term(row_start, row_count):
        return jnp.einsum("rkf,kdf->rkd", pre_grad, w_in, preferred_element_type=jnp.float32)

    zero_full = jnp.zeros_like(b_out)
    slot_in_grad = send_home(
        input_term, row_total, n_expert, quarter, local_experts, width, zero_full
    )
    offset = lax.axis_index("hidden") * quarter
    mine_tokens = lax.dynamic_slice_in_dim(tokens, offset, quarter, 0)
    mine_grad = lax.dynamic_slice_in_dim(out_grad, offset, quarter, 0)
    mine_dispatch = lax.dynamic_slice_in_dim(dispatch, offset, quarter, 0)
    mine_combine = lax.dynamic_slice_in_dim(combine, offset, quarter, 0)
    comb_grad = jnp.einsum("btd,bsd->bts", mine_grad, slot_out, preferred_element_type=jnp.float32)
    disp_grad = jnp.einsum(
        "btd,bsd->bts", mine_tokens, slot_in_grad, preferred_element_type=jnp.float32
    )
    comb_wide = mine_combine.astype(jnp.float32)
    disp_wide = mine_dispatch.astype(jnp.float32)
    logit_grad = comb_wide * (comb_grad - jnp.sum(comb_wide * comb_grad, axis=2, keepdims=True))
    logit_grad = logit_grad + disp_wide * (
        disp_grad - jnp.sum(disp_wide * disp_grad, axis=1, keepdims=True)
    )
    logit_grad = logit_grad.astype(jnp.bfloat16)
    token_grad = jnp.einsum(
        "bts,bsd->btd", mine_dispatch, slot_in_grad, preferred_element_type=jnp.float32
    )
    token_grad = token_grad + jnp.einsum(
        "bts,ds->btd", logit_grad, slot_keys, preferred_element_type=jnp.float32
    )
    return token_grad.astype(jnp.bfloat16)


def solution(mesh):
    return jax.shard_map(
        local,
        mesh=mesh,
        in_specs=(
            P("expert", None, None),
            P(),
            P("expert", None, "hidden"),
            P("expert", "hidden"),
            P("expert", "hidden", None),
            P(),
            P("expert", None, None),
        ),
        out_specs=P(("expert", "hidden"), None, None),
        check_vma=False,
    )
```

profile of v0, /device:TPU:1, one launch (start us, length us, event | category | flops | bytes accessed | tf_op | source)
XLA Modules:
  0.0 224.5 jit_solution(5408577604933671505)
XLA Ops:
  6.5 0.0 copy-start
  6.5 0.9 copy-done
  7.5 2.7 %fusion.139 = (f32[4,196]{1,0:T(4,128)S(1)}, f32[4,196,128]{2,1,0:T(8,128)S(1)}) fusion(bf16[1024,128]{1,0:T(8,128)(2,1)S(1)} %copy-done, bf16[4,196,1024]{2,0,1:T(4,128)(2,1)} %param.7), kind=kOutput, calls=%fused_computation.157 | convolution fusion | flops 205721728 | bytes 2272320 | tf_op jit(solution)/shard_map/sub | solution.py:35
  10.2 0.2 divide_convert_fusion
  10.4 0.0 copy-start.5
  10.4 0.7 copy-done.5
  11.1 0.0 copy-done.1
  11.1 1.2 fusion.25
  12.3 0.0 copy-start.2
  12.3 1.8 copy.43
  14.1 15.4 %all-to-all-start = ((bf16[4,1,128,1024]{3,0,1,2:T(4,128)(2,1)}), bf16[4,1,128,1024]{3,0,1,2:T(4,128)(2,1)}, u32[]{:S(2)}, u32[]{:S(2)}) async-start(bf16[4,1,128,1024]{3,0,1,2:T(4,128)(2,1)} %copy.43), calls=%async_computation | async-start | bytes 2097152 | tf_op jit(solution)/shard_map/all_to_all | solution.py:45
  29.5 0.0 copy-done.2
  29.5 1.8 fusion.138
  31.3 1.0 divide_convert_fusion.1
  32.3 0.0 copy-start.3
  32.4 0.7 copy-done.3
  33.0 1.2 fusion.26
  34.2 1.8 copy.47
  36.1 22.2 %all-to-all-done = bf16[4,1,128,1024]{3,0,1,2:T(4,128)(2,1)} async-done(((bf16[4,1,128,1024]{3,0,1,2:T(4,128)(2,1)}), bf16[4,1,128,1024]{3,0,1,2:T(4,128)(2,1)}, u32[]{:S(2)}, u32[]{:S(2)}) %all-to-all-start) | async-done | bytes 1048608 | tf_op jit(solution)/shard_map/all_to_all | solution.py:45
  58.3 6.6 %all-to-all-start.1 = ((bf16[4,1,128,1024]{3,0,1,2:T(4,128)(2,1)}), bf16[4,1,128,1024]{3,0,1,2:T(4,128)(2,1)}, u32[]{:S(2)}, u32[]{:S(2)}) async-start(bf16[4,1,128,1024]{3,0,1,2:T(4,128)(2,1)} %copy.47), calls=%async_computation.1 | async-start | bytes 2097152 | tf_op jit(solution)/shard_map/all_to_all | solution.py:44
  64.9 0.2 reduce-scatter.3.cloned.1.call-start
  65.2 2.5 %copy.44 = bf16[4,1,128,1024]{3,2,0,1:T(8,128)(2,1)} copy(bf16[4,1,128,1024]{3,0,1,2:T(4,128)(2,1)} %all-to-all-done) | data formatting | bytes 2097152 | tf_op jit(solution)/shard_map/all_to_all | solution.py:45
  67.7 2.3 %reshape.90 = bf16[256,2,1024]{2,1,0:T(2,128)(2,1)} reshape(bf16[4,1,128,1024]{3,2,0,1:T(8,128)(2,1)} %copy.44) | data formatting | bytes 2097152 | tf_op jit(solution)/shard_map/reshape | solution.py:51
  69.9 18.4 %all-to-all-done.1 = bf16[4,1,128,1024]{3,0,1,2:T(4,128)(2,1)} async-done(((bf16[4,1,128,1024]{3,0,1,2:T(4,128)(2,1)}), bf16[4,1,128,1024]{3,0,1,2:T(4,128)(2,1)}, u32[]{:S(2)}, u32[]{:S(2)}) %all-to-all-start.1) | async-done | bytes 1048608 | tf_op jit(solution)/shard_map/all_to_all | solution.py:44
  88.3 2.6 %copy.48 = bf16[4,1,128,1024]{3,2,0,1:T(8,128)(2,1)} copy(bf16[4,1,128,1024]{3,0,1,2:T(4,128)(2,1)} %all-to-all-done.1) | data formatting | bytes 2097152 | tf_op jit(solution)/shard_map/all_to_all | solution.py:44
  90.9 2.3 %reshape.92 = bf16[256,2,1024]{2,1,0:T(2,128)(2,1)} reshape(bf16[4,1,128,1024]{3,2,0,1:T(8,128)(2,1)} %copy.48) | data formatting | bytes 2097152 | tf_op jit(solution)/shard_map/reshape | solution.py:50
  93.1 5.1 %fusion.34 = f32[2,256,1024]{2,1,0:T(8,128)} fusion(bf16[2,1024,1024]{2,1,0:T(8,128)(2,1)} %param.9, bf16[256,2,1024]{2,1,0:T(2,128)(2,1)} %reshape.92), kind=kOutput, calls=%fused_computation.49 | convolution fusion | flops 1073741824 | bytes 7340032 | tf_op jit(solution)/shard_map/rkd,kdf->rkf/dot_general | solution.py:53
  98.3 0.0 copy-done.8
  98.3 8.0 %convolution_convert_fusion.1 = bf16[2,256,1024]{2,1,0:T(8,128)(2,1)} fusion(bf16[2,1024,1024]{2,1,0:T(8,128)(2,1)} %param.9, f32[2,256,1024]{2,1,0:T(8,128)} %fusion.34, bf16[2,1024,1024]{2,1,0:T(8,128)(2,1)} %param.11, bf16[256,2,1024]{2,1,0:T(2,128)(2,1)} %reshape.90, f32[2,1024]{1,0:T(2,128)S(1)} %copy-done.8), kind=kOutput, calls=%fused_computation.37 | convolution fusion | flops 2153775104 | bytes 12591104 | tf_op jit(solution)/shard_map/rkf,kdf->rkd/dot_general | solution.py:65
  106.3 2.0 copy.50
  108.4 26.0 %all_to_all.42 = bf16[4,64,1,2,1024]{4,0,3,2,1:T(4,128)(2,1)S(1)} all-to-all(bf16[4,64,1,2,1024]{4,0,3,2,1:T(4,128)(2,1)S(1)} %copy.50), channel_id=1, replica_groups=mesh['expert'=64,'hidden'=4] {'expert'}, dimensions={1} | all-to-all | bytes 2097152 | tf_op jit(solution)/shard_map/all_to_all | solution.py:18
  134.3 1.3 copy.51
  135.6 0.0 reduce-scatter.3.cloned.1.call-update
  135.7 0.0 reduce-scatter.5.cloned.1.call-start
  135.7 8.3 %convolution_convert_fusion = bf16[2,256,1024]{2,1,0:T(8,128)(2,1)S(1)} fusion(bf16[2,1024,1024]{2,1,0:T(8,128)(2,1)} %param.11, f32[2,256,1024]{2,1,0:T(8,128)} %fusion.34, f32[2,1024]{1,0:T(2,128)S(1)} %copy-done.8), kind=kOutput, calls=%fused_computation.36 | convolution fusion | flops 1108869120 | bytes 7348224 | tf_op jit(solution)/shard_map/rkf,kfd->rkd/dot_general | solution.py:58
  144.0 0.8 copy.53
  144.8 24.7 %all_to_all.43 = bf16[4,64,1,2,1024]{4,0,3,2,1:T(4,128)(2,1)S(1)} all-to-all(bf16[4,64,1,2,1024]{4,0,3,2,1:T(4,128)(2,1)S(1)} %copy.53), channel_id=1, replica_groups=mesh['expert'=64,'hidden'=4] {'expert'}, dimensions={1} | all-to-all | bytes 2097152 | tf_op jit(solution)/shard_map/all_to_all | solution.py:18
  169.5 1.3 copy.54
  170.8 0.0 reduce-scatter.5.cloned.1.call-update
  170.8 1.7 copy.42
  172.5 1.7 copy.41
  174.2 4.7 %reduce-scatter.3.cloned.1.call-done = bf16[1,1,1,128,1024]{4,3,2,1,0:T(8,128)(2,1)} async-done(((bf16[4,1,1,128,1024]{4,3,2,1,0:T(8,128)(2,1)}), bf16[1,1,1,128,1024]{4,3,2,1,0:T(8,128)(2,1)}) %reduce-scatter.3.cloned.1.call-update) | async-done | bytes 262160 | tf_op jit(solution)/shard_map/reduce_scatter | solution.py:19
  178.8 1.4 fusion.87
  180.2 1.2 fusion.80
  181.4 33.7 %reduce-scatter.5.cloned.1.call-done = bf16[1,1,1,128,1024]{4,3,2,1,0:T(8,128)(2,1)} async-done(((bf16[4,1,1,128,1024]{4,3,2,1,0:T(8,128)(2,1)}), bf16[1,1,1,128,1024]{4,3,2,1,0:T(8,128)(2,1)}) %reduce-scatter.5.cloned.1.call-update) | async-done | bytes 262160 | tf_op jit(solution)/shard_map/reduce_scatter | solution.py:19
  215.1 0.0 copy-done.6
  215.1 1.4 fusion.84
  216.6 1.1 fusion.30
  (7 shorter events, 0.0 us)
Async XLA Ops:
  6.5 1.0 copy-start
  6.5 4.5 %copy-start.1 = (bf16[4,196,1024]{2,0,1:T(4,128)(2,1)S(1)}, bf16[4,196,1024]{2,0,1:T(4,128)(2,1)}, u32[]{:S(2)}) copy-start(bf16[4,196,1024]{2,0,1:T(4,128)(2,1)} %param.13) | copy-start | bytes 4816900
  10.4 0.7 copy-start.5
  12.3 17.2 %copy-start.2 = (bf16[4,196,1024]{2,0,1:T(4,128)(2,1)S(1)}, bf16[4,196,1024]{2,0,1:T(4,128)(2,1)}, u32[]{:S(2)}) copy-start(bf16[4,196,1024]{2,0,1:T(4,128)(2,1)} %param.7) | copy-start | bytes 4816900
  14.1 44.2 %all-to-all-start = ((bf16[4,1,128,1024]{3,0,1,2:T(4,128)(2,1)}), bf16[4,1,128,1024]{3,0,1,2:T(4,128)(2,1)}, u32[]{:S(2)}, u32[]{:S(2)}) async-start(bf16[4,1,128,1024]{3,0,1,2:T(4,128)(2,1)} %copy.43), calls=%async_computation | async-start | bytes 2097152 | tf_op jit(solution)/shard_map/all_to_all | solution.py:45
  32.3 0.7 copy-start.3
  58.3 30.0 %all-to-all-start.1 = ((bf16[4,1,128,1024]{3,0,1,2:T(4,128)(2,1)}), bf16[4,1,128,1024]{3,0,1,2:T(4,128)(2,1)}, u32[]{:S(2)}, u32[]{:S(2)}) async-start(bf16[4,1,128,1024]{3,0,1,2:T(4,128)(2,1)} %copy.47), calls=%async_computation.1 | async-start | bytes 2097152 | tf_op jit(solution)/shard_map/all_to_all | solution.py:44
  64.9 113.9 %reduce-scatter.3.cloned.1.call-start = ((), (), s32[]{:S(2)}) async-start(), calls=%async_computation.6 | async-start | bytes 1310720 | tf_op jit(solution)/shard_map/reduce_scatter | solution.py:19
  93.1 5.2 %copy-start.8 = (f32[2,1024]{1,0:T(2,128)S(1)}, f32[2,1024]{1,0:T(2,128)}, u32[]{:S(2)}) copy-start(f32[2,1024]{1,0:T(2,128)} %param.10) | copy-start | bytes 24580
  135.7 79.5 %reduce-scatter.5.cloned.1.call-start = ((), (), s32[]{:S(2)}) async-start(), calls=%async_computation.7 | async-start | bytes 1310720 | tf_op jit(solution)/shard_map/reduce_scatter | solution.py:19
  172.5 6.3 %copy-start.4 = (bf16[4,196,128]{2,1,0:T(8,128)(2,1)S(1)}, bf16[4,196,128]{2,1,0:T(8,128)(2,1)}, u32[]{:S(2)}) copy-start(bf16[4,196,128]{2,1,0:T(8,128)(2,1)} %copy-done.3) | copy-start | bytes 602116
  172.5 42.6 %copy-start.6 = (bf16[4,196,128]{2,1,0:T(8,128)(2,1)S(1)}, bf16[4,196,128]{2,1,0:T(8,128)(2,1)}, u32[]{:S(2)}) copy-start(bf16[4,196,128]{2,1,0:T(8,128)(2,1)} %copy-done.5) | copy-start | bytes 602116
  174.2 40.9 %copy-start.7 = (f32[128,1024]{1,0:T(8,128)S(1)}, f32[128,1024]{1,0:T(8,128)}, u32[]{:S(2)}) copy-start(f32[128,1024]{1,0:T(8,128)} %param.12) | copy-start | bytes 1572868
Sparse Core Ops, SparseCore 0:
  135.8 43.0 reduce-scatter.2
  181.4 33.6 reduce-scatter.4
where the time goes:
time: 225 us
  waiting for transfers between devices  79 us (35%)
  blocking collectives  50.7 us (23%)
  matrix products  33.5 us (15%)
  local copies, waits for them, and re-layouts  24.4 us (11%)
  starting transfers between devices  22.2 us (10%)
  between operations  13.5 us (6%)
    all_to_all x2, blocking collectives, send_home(): lax.all_to_all(term, 'expert', split_axis=1, concat_axis=3, tiled=True)  50.7 us
    reduce_scatter x2, waiting for transfers between devices, send_home(): lax.psum_scatter(moved.astype(jnp.float32).astype(jnp.bfloat16), 'hidden'...  38.4 us
    all_to_all x1, waiting for transfers between devices, local(): lax.all_to_all(slot_grad.reshape(grouped), 'expert', split_axis=2, concat...  22.2 us
    all_to_all x1, waiting for transfers between devices, local(): lax.all_to_all(slot_in.reshape(grouped), 'expert', split_axis=2, concat_a...  18.4 us
    all_to_all x1, starting transfers between devices, local(): lax.all_to_all(slot_grad.reshape(grouped), 'expert', split_axis=2, concat...  15.4 us
    dot_general x1, matrix products, output_term(): jnp.einsum('rkf,kfd->rkd', hidden_act, w_out, preferred_element_type=jnp....  8.29 us
    dot_general x1, matrix products, input_term(): jnp.einsum('rkf,kdf->rkd', pre_grad, w_in, preferred_element_type=jnp.flo...  8.04 us
    all_to_all x1, starting transfers between devices, local(): lax.all_to_all(slot_in.reshape(grouped), 'expert', split_axis=2, concat_a...  6.59 us
  transfers between devices with their start and end apart: 4, of which 4 were waited for; matrix products, arithmetic and copies ran while one was open for 12% of the time, Pallas kernels for 0%

commit v1 on v0

v1 whole, which is shorter than its diff:
```python
import functools

import jax
import jax.numpy as jnp
from jax import lax
from jax.experimental import pallas as pl
from jax.experimental.pallas import tpu as pltpu
from jax.sharding import PartitionSpec as P

BF = jnp.bfloat16
F32 = jnp.float32
MESH = pl.DeviceIdType.MESH
NT = (((1,), (1,)), ((), ()))
TN = (((0,), (0,)), ((), ()))


def mm(a, b):
    return jnp.dot(a, b, preferred_element_type=F32)


def nt(a, b):
    return lax.dot_general(a, b, NT, preferred_element_type=F32)


def tn(a, b):
    return lax.dot_general(a, b, TN, preferred_element_type=F32)


def onehot(shape, test):
    rows = lax.broadcasted_iota(jnp.int32, shape, 0)
    cols = lax.broadcasted_iota(jnp.int32, shape, 1)
    return jnp.where(test(rows, cols), 1.0, 0.0)


def kernel(
    tok_h, grad_h, keys_h, win_h, bin_h, wout_h, bout_h,
    out_ref,
    tok4, grad4, tok, grad, keys, win, wout, bin_, bout,
    send, rows0, rows1, slope, inter, part, fromcore, frompair, home,
    own_tok, own_grad, own_disp, own_comb, comb_all,
    load_sem, put_sem, got_sem, self_sem, fwd_sem, fgot_sem, cput_sem, cgot_sem,
    rput_sem, rgot_sem, zput_sem, zgot_sem, hput_sem, hgot_sem, hself_sem,
):
    e = lax.axis_index("expert")
    h = lax.axis_index("hidden")
    x, y, p = e // 16, (e // 4) % 4, e % 4
    zl, c = h // 2, h % 2
    n_slots, positions = 64, tok4.shape[0]
    rows_all = positions * 4
    rows = (rows0, rows1)

    def expert_at(dx, dy, dp):
        return ((x + dx) % 4) * 16 + ((y + dy) % 4) * 4 + (p + dp) % 4

    loads = [
        pltpu.make_async_copy(src, dst, load_sem.at[i])
        for i, (src, dst) in enumerate((
            (tok_h, tok4), (keys_h, keys), (grad_h, grad4), (win_h, win), (bin_h, bin_),
            (wout_h, wout), (bout_h, bout),
        ))
    ]
    for copy in loads:
        copy.start()

    barrier = pltpu.get_barrier_semaphore()

    def greet(expert, hidden):
        pl.semaphore_signal(barrier, inc=1, device_id=(expert, hidden), device_id_type=MESH)

    def greet_step(i, carry):
        dx, dy = i // 4, i % 4
        greet(expert_at(dx, dy, 1), c)
        greet(expert_at(dx, dy, 3), 2 + c)
        greet(expert_at(dx, dy, 2), 2 * (1 - zl) + c)
        return carry

    def greet_own(i, carry):
        greet(expert_at(i // 4, i % 4, 0), h)
        return carry

    lax.fori_loop(0, 16, greet_step, 0)
    lax.fori_loop(1, 16, greet_own, 0)
    greet(e, 2 * (1 - zl) + c)
    greet(e, 2 * zl + 1 - c)

    loads[0].wait()
    loads[1].wait()
    tok[...] = tok4[...].reshape(rows_all, tok4.shape[2])
    logits = mm(tok[...], keys[...])
    folded = logits.reshape(rows_all // 8, 8, logits.shape[1])
    top = jnp.max(folded, axis=0)
    top = jnp.maximum(top, pltpu.roll(top, 4, 0))
    weight = jnp.exp(folded - top[None])
    total = jnp.sum(weight, axis=0)
    total = total + pltpu.roll(total, 4, 0)
    dispatch = (weight / total[None]).reshape(rows_all, logits.shape[1]).astype(BF)
    weight = jnp.exp(logits - jnp.max(logits, axis=1, keepdims=True))
    combine = (weight / jnp.sum(weight, axis=1, keepdims=True)).astype(BF)
    comb_all[...] = combine
    spread = onehot((128, 256), lambda r, q: q // 2 == r).astype(BF)
    image = lax.broadcasted_iota(jnp.int32, (rows_all, 256), 0) % 4
    wanted = c + 2 * (lax.broadcasted_iota(jnp.int32, (rows_all, 256), 1) % 2)

    def slots(scores, values):
        wide = jnp.where(image == wanted, mm(scores, spread), 0.0).astype(BF)
        return tn(wide, values).astype(BF).reshape(64, 2, 2, values.shape[1])

    def put(t, expert, hidden, slot, group):
        return pltpu.make_async_remote_copy(
            src_ref=send.at[t, expert], dst_ref=rows[t].at[c, slot],
            send_sem=put_sem.at[t], recv_sem=got_sem.at[t, group],
            device_id=(expert, hidden), device_id_type=MESH,
        )

    def odd_even(b, par):
        dx = b // 2
        return dx, 2 * (b % 2) + (dx + par) % 2

    def send_all(t):
        def far(b, carry):
            dx, dy = odd_even(b, 1 - zl)
            put(t, expert_at(dx, dy, 2), 2 * (1 - zl) + c, 16 + 8 * (1 - zl) + b, 1).start()
            return carry

        def near(i, carry):
            put(t, expert_at(i // 4, i % 4, 3 - 2 * zl), 2 * (1 - zl) + c, 32 * (1 - zl) + i, 0).start()
            return carry

        def level(i, carry):
            put(t, expert_at(i // 4, i % 4, 0), h, 48 + i, 2).start()
            return carry

        pltpu.make_async_copy(send.at[t, e], rows[t].at[c, 48], self_sem.at[t]).start()
        lax.fori_loop(0, 8, far, 0)
        lax.fori_loop(0, 16, near, 0)
        lax.fori_loop(1, 16, level, 0)

    def wait_for(ref, sem):
        pltpu.make_async_copy(ref, ref, sem).wait()

    send[0] = slots(dispatch, tok[...])
    pl.semaphore_wait(barrier, 65)
    send_all(0)
    loads[2].wait()
    grad[...] = grad4[...].reshape(rows_all, grad4.shape[2])
    send[1] = slots(comb_all[...], grad[...])
    send_all(1)

    pick = onehot((positions, rows_all), lambda r, q: q == 4 * r + h).astype(BF)
    own_tok[...] = mm(pick, tok[...]).astype(BF)
    own_grad[...] = mm(pick, grad[...]).astype(BF)
    own_disp[...] = mm(pick, dispatch)
    own_comb[...] = mm(pick, comb_all[...])
    for copy in loads[3:]:
        copy.wait()

    pair = (e, 2 * (1 - zl) + c)
    mate = (e, 2 * zl + 1 - c)
    base_a = 32 * zl
    base_b = 16 + 8 * zl
    pair_a = 32 * (1 - zl)
    pair_b = 16 + 8 * (1 - zl)

    def share(t, which, start, count):
        piece = rows[t].at[c, pl.ds(start, count)]
        pltpu.make_async_remote_copy(
            src_ref=piece, dst_ref=piece, send_sem=cput_sem.at[t, which], recv_sem=cgot_sem.at[t, which],
            device_id=mate, device_id_type=MESH,
        ).start()

    def forward(t, which, start, count):
        piece = rows[t].at[c, pl.ds(start, count)]
        pltpu.make_async_remote_copy(
            src_ref=piece, dst_ref=piece, send_sem=fwd_sem.at[t, which], recv_sem=fgot_sem.at[t, which],
            device_id=pair, device_id_type=MESH,
        ).start()

    def gather_rows(t):
        wait_for(rows[t].at[c, pl.ds(base_b, 8)], got_sem.at[t, 1])
        forward(t, 1, base_b, 8)
        share(t, 1, base_b, 8)
        wait_for(rows[t].at[c, pl.ds(base_a, 16)], got_sem.at[t, 0])
        forward(t, 0, base_a, 16)
        share(t, 0, base_a, 16)
        wait_for(rows[t].at[c, pl.ds(49, 15)], got_sem.at[t, 2])
        pltpu.make_async_copy(send.at[t, e], rows[t].at[c, 48], self_sem.at[t]).wait()
        share(t, 2, 48, 16)
        wait_for(rows[t].at[c, pl.ds(pair_b, 8)], fgot_sem.at[t, 1])
        share(t, 3, pair_b, 8)
        wait_for(rows[t].at[c, pl.ds(pair_a, 16)], fgot_sem.at[t, 0])
        share(t, 4, pair_a, 16)
        wait_for(rows[t].at[c, pl.ds(0, 8)], cgot_sem.at[t, 1])
        wait_for(rows[t].at[c, pl.ds(0, 16)], cgot_sem.at[t, 0])
        wait_for(rows[t].at[c, pl.ds(0, 16)], cgot_sem.at[t, 2])
        wait_for(rows[t].at[c, pl.ds(0, 8)], cgot_sem.at[t, 3])
        wait_for(rows[t].at[c, pl.ds(0, 16)], cgot_sem.at[t, 4])

    width = tok4.shape[2]

    def expert_rows(t, k):
        return rows[t][:, :, k].reshape(256, width)

    def core_copy(t):
        return pltpu.make_async_remote_copy(
            src_ref=part.at[t, 1 - c], dst_ref=fromcore.at[t], send_sem=rput_sem.at[t], recv_sem=rgot_sem.at[t],
            device_id=mate, device_id_type=MESH,
        )

    def pair_copies(t):
        sent = (
            part.at[t, c, pl.ds(32 * (1 - zl), 16)],
            part.at[t, c, pl.ds(16, 16), pl.ds(zl, 1)],
            part.at[t, c, pl.ds(48, 16), pl.ds(1 - zl, 1)],
        )
        land = (
            frompair.at[t, pl.ds(0, 16)],
            frompair.at[t, pl.ds(16, 16), pl.ds(0, 1)],
            frompair.at[t, pl.ds(16, 16), pl.ds(1, 1)],
        )
        return [
            pltpu.make_async_remote_copy(
                src_ref=s, dst_ref=d, send_sem=zput_sem.at[t, i], recv_sem=zgot_sem.at[t, i],
                device_id=pair, device_id_type=MESH,
            )
            for i, (s, d) in enumerate(zip(sent, land))
        ]

    def add_core(t):
        core_copy(t).wait_recv()
        mine = part[t, c]
        part[t, c] = (mine.astype(F32) + fromcore[t].astype(F32)).astype(BF)

    def add_pair(t):
        for copy in pair_copies(t):
            copy.wait_recv()
        first = part[t, c, pl.ds(32 * zl, 16)].astype(F32)
        frompair[t, 0:16] = (frompair[t, 0:16].astype(F32) + first).astype(BF)
        second = part[t, c, 16:32, pl.ds(1 - zl, 1)].astype(F32)
        frompair[t, 16:32, 0:1] = (frompair[t, 16:32, 0:1].astype(F32) + second).astype(BF)
        third = part[t, c, 48:64, pl.ds(zl, 1)].astype(F32)
        frompair[t, 16:32, 1:2] = (frompair[t, 16:32, 1:2].astype(F32) + third).astype(BF)

    def go_home(t):
        def put_home(slot, j, expert, hidden):
            pltpu.make_async_remote_copy(
                src_ref=frompair.at[t, slot, j], dst_ref=home.at[t, e], send_sem=hput_sem.at[t],
                recv_sem=hgot_sem.at[t], device_id=(expert, hidden), device_id_type=MESH,
            ).start()

        def far(b, carry):
            for par in (0, 1):
                dx, dy = odd_even(b, par)
                put_home(16 + 8 * par + b, 0, expert_at(4 - dx, 4 - dy, 2), 2 * (1 - zl) + c)
            return carry

        def near(i, carry):
            expert = expert_at(4 - i // 4, 4 - i % 4, 3 - 2 * zl)
            put_home(i, 0, expert, c)
            put_home(i, 1, expert, 2 + c)
            return carry

        def level(i, carry):
            put_home(16 + i, 1, expert_at(4 - i // 4, 4 - i % 4, 0), h)
            return carry

        pltpu.make_async_copy(frompair.at[t, 16, 1], home.at[t, e], hself_sem.at[t]).start()
        lax.fori_loop(0, 8, far, 0)
        lax.fori_loop(0, 16, near, 0)
        lax.fori_loop(1, 16, level, 0)

    def interleave(k, product):
        for n in range(width // 128):
            inter[n, pl.ds(k, 256, 2), :] = product[:, 128 * n : 128 * n + 128]

    def pack(t):
        both = jnp.concatenate([inter[n] for n in range(width // 128)], axis=1)
        part[t] = both.astype(BF).reshape(2, n_slots, 2, 2, width)

    gather_rows(0)
    for k in range(2):
        pre = mm(expert_rows(0, k), win[k]) + bin_[k : k + 1]
        half = 0.5 * (1.0 + lax.erf(pre * 0.7071067811865476))
        slope[k] = half + pre * jnp.exp(-0.5 * pre * pre) * 0.3989422804014327
        interleave(k, mm((pre * half).astype(BF), wout[k]))
    pack(0)
    core_copy(0).start()
    add_core(0)
    for copy in pair_copies(0):
        copy.start()

    gather_rows(1)
    add_pair(0)
    go_home(0)
    for k in range(2):
        pre_grad = (nt(expert_rows(1, k), wout[k]) * slope[k]).astype(BF)
        interleave(k, nt(pre_grad, win[k]))
    pack(1)
    core_copy(1).start()
    add_core(1)
    for copy in pair_copies(1):
        copy.start()
    add_pair(1)
    go_home(1)

    def wait_home(t):
        wait_for(home.at[t, pl.ds(0, 63)], hgot_sem.at[t])
        pltpu.make_async_copy(frompair.at[t, 16, 1], home.at[t, e], hself_sem.at[t]).wait()

    wait_home(0)
    slot_out = (home[0].reshape(128, width).astype(F32) + bout[...]).astype(BF)
    comb = own_comb[...]
    disp = own_disp[...]
    comb_grad = nt(own_grad[...], slot_out)
    comb_term = comb * (comb_grad - jnp.sum(comb * comb_grad, axis=1, keepdims=True))
    wait_home(1)
    slot_in_grad = home[1].reshape(128, width)
    disp_grad = nt(own_tok[...], slot_in_grad)
    logit_grad = comb_term + disp * (disp_grad - jnp.sum(disp * disp_grad, axis=0, keepdims=True))
    result = mm(disp.astype(BF), slot_in_grad) + nt(logit_grad.astype(BF), keys[...])
    out_ref[...] = result.astype(BF)

    for t in range(2):
        wait_for(send.at[t, pl.ds(0, 39)], put_sem.at[t])
        wait_for(rows[t].at[0, pl.ds(0, 16)], fwd_sem.at[t, 0])
        wait_for(rows[t].at[0, pl.ds(0, 8)], fwd_sem.at[t, 1])
        for which, count in enumerate((16, 8, 16, 8, 16)):
            wait_for(rows[t].at[0, pl.ds(0, count)], cput_sem.at[t, which])
        core_copy(t).wait_send()
        for copy in pair_copies(t):
            copy.wait_send()
        wait_for(home.at[t, pl.ds(0, 63)], hput_sem.at[t])


def local(tokens, slot_keys, w_in, b_in, w_out, b_out, out_grad):
    images, positions, width = tokens.shape
    units = w_in.shape[2]
    slots = slot_keys.shape[1]
    anyspec = pl.BlockSpec(memory_space=pl.ANY)
    dma = pltpu.SemaphoreType.DMA
    out = pl.pallas_call(
        kernel,
        out_shape=jax.ShapeDtypeStruct((positions, width), BF),
        in_specs=[anyspec] * 7,
        out_specs=pl.BlockSpec(memory_space=pltpu.VMEM),
        scratch_shapes=[
            pltpu.VMEM((positions, images, width), BF),
            pltpu.VMEM((positions, images, width), BF),
            pltpu.VMEM((positions * images, width), BF),
            pltpu.VMEM((positions * images, width), BF),
            pltpu.VMEM((width, slots), BF),
            pltpu.VMEM((2, width, units), BF),
            pltpu.VMEM((2, units, width), BF),
            pltpu.VMEM((2, units), F32),
            pltpu.VMEM((slots, width), F32),
            pltpu.VMEM((2, 64, 2, 2, width), BF),
            pltpu.VMEM((2, 64, 2, 2, width), BF),
            pltpu.VMEM((2, 64, 2, 2, width), BF),
            pltpu.VMEM((2, 256, units), F32),
            pltpu.VMEM((width // 128, 512, 128), F32),
            pltpu.VMEM((2, 2, 64, 2, 2, width), BF),
            pltpu.VMEM((2, 64, 2, 2, width), BF),
            pltpu.VMEM((2, 32, 2, 2, width), BF),
            pltpu.VMEM((2, 64, 2, width), BF),
            pltpu.VMEM((positions, width), BF),
            pltpu.VMEM((positions, width), BF),
            pltpu.VMEM((positions, slots), F32),
            pltpu.VMEM((positions, slots), F32),
            pltpu.VMEM((positions * images, slots), BF),
            dma((7,)), dma((2,)), dma((2, 3)), dma((2,)), dma((2, 2)), dma((2, 2)), dma((2, 5)), dma((2, 5)),
            dma((2,)), dma((2,)), dma((2, 3)), dma((2, 3)), dma((2,)), dma((2,)), dma((2,)),
        ],
        compiler_params=pltpu.CompilerParams(
            collective_id=0, has_side_effects=True, vmem_limit_bytes=58 * 1024 * 1024
        ),
        name="moe_input_grad",
    )(
        jnp.transpose(tokens, (1, 0, 2)), jnp.transpose(out_grad, (1, 0, 2)), slot_keys, w_in, b_in, w_out, b_out
    )
    return out[None]


def solution(mesh):
    return jax.shard_map(
        local,
        mesh=mesh,
        in_specs=(
            P("expert", None, None),
            P(),
            P("expert", None, "hidden"),
            P("expert", "hidden"),
            P("expert", "hidden", None),
            P(),
            P("expert", None, None),
        ),
        out_specs=P(("expert", "hidden"), None, None),
        check_vma=False,
    )
```

time: 225 us -> 71.6 us (0.32)
  waiting for transfers between devices: 79 us -> 0 us
  Pallas kernels: 0 us -> 69.7 us
  blocking collectives: 50.7 us -> 0 us
  matrix products: 33.5 us -> 0 us
  local copies, waits for them, and re-layouts: 24.4 us -> 1.78 us
  starting transfers between devices: 22.2 us -> 0 us
  between operations: 13.5 us -> 0.01 us
    pallas_call x0 -> x1, Pallas kernels: none -> 69.7 us  [local(): pl.pallas_call(kernel, out_shape=jax.ShapeDtypeStruct((positions, width),...]
    all_to_all x2 -> x0, blocking collectives: 50.7 us -> none  [send_home(): lax.all_to_all(term, 'expert', split_axis=1, concat_axis=3, tiled=True)]
    all_to_all x2 -> x0, waiting for transfers between devices: 40.6 us -> none  [the longest x1 22.2 us: local(): lax.all_to_all(slot_grad.reshape(grouped), 'expert', split_axis=2, concat...]
    reduce_scatter x2 -> x0, waiting for transfers between devices: 38.4 us -> none  [send_home(): lax.psum_scatter(moved.astype(jnp.float32).astype(jnp.bfloat16), 'hidden'...]
    dot_general x9 -> x0, matrix products: 29 us -> none  [the longest x1 8.29 us: output_term(): jnp.einsum('rkf,kfd->rkd', hidden_act, w_out, preferred_element_type=jnp....]
    all_to_all x2 -> x0, starting transfers between devices: 21.9 us -> none  [the longest x1 15.4 us: local(): lax.all_to_all(slot_grad.reshape(grouped), 'expert', split_axis=2, concat...]
    reshape x6 -> x0, local copies, waits for them, and re-layouts: 11 us -> none  [the longest x2 2.85 us: send_home(): term = term.reshape(n_hidden, n_expert, quarter, local_experts, width)]
    all_to_all x4 -> x0, local copies, waits for them, and re-layouts: 7.67 us -> none  [the longest x2 2.58 us: send_home(): lax.all_to_all(term, 'expert', split_axis=1, concat_axis=3, tiled=True)]
  transfers between devices with their start and end apart: 4 -> 0, of which waited for: 4 -> 0; matrix products, arithmetic and copies ran while one was open for 12% -> 0% of each run, Pallas kernels for 0% -> 0%
where the time goes in v1:
time: 71.6 us; the launch traced here: 71.5 us
  Pallas kernels  69.7 us (97%)
  local copies, waits for them, and re-layouts  1.78 us (2%)
    pallas_call x1, Pallas kernels, local(): pl.pallas_call(kernel, out_shape=jax.ShapeDtypeStruct((positions, width),...  69.7 us
    unnamed x1, local copies, waits for them, and re-layouts  1.78 us

profile of v1, /device:TPU:1, one launch (start us, length us, event | category | flops | bytes accessed | tf_op | source)
XLA Modules:
  0.0 71.5 jit_solution(7640805634047044929)
XLA Ops:
  0.0 69.7 %moe_input_grad.1 = bf16[196,1024]{1,0:T(8,128)(2,1)} custom-call(bf16[196,4,1024]{2,1,0:T(4,128)(2,1)} %bitcast.4, bf16[196,4,1024]{2,1,0:T(4,128)(2,1)} %bitcast.5, bf16[1024,128]{1,0:T(8,128)(2,1)} %keys_h.1, bf16[2,1024,1024]{2,1,0:T(8,128)(2,1)} %win_h.1, f32[2,1024]{1,0:T(2,128)} %bin_h.1, bf16[2,1024,1024]{2,1,0:T(8,128)(2,1)} %wout_h.1, ...), custom_call_target="tpu_custom_call" | custom-call | tf_op jit(solution)/shard_map/moe_input_grad/pallas_call | solution.py:340
  69.7 1.8 %copy.9 = bf16[1,196,1024]{2,1,0:T(8,128)(2,1)} copy(bf16[1,196,1024]{2,1,0:T(8,128)(2,1)} %bitcast.3) | data formatting | bytes 802816

commit v2 on v1

--- a/solution.py
+++ b/solution.py
@@ -36,7 +36,7 @@
     tok_h, grad_h, keys_h, win_h, bin_h, wout_h, bout_h,
     out_ref,
     tok4, grad4, tok, grad, keys, win, wout, bin_, bout,
-    send, rows0, rows1, slope, inter, part, fromcore, frompair, home,
+    send, rows0, rows1, slope, act, inter, part, fromcore, frompair, home,
     own_tok, own_grad, own_disp, own_comb, comb_all,
     load_sem, put_sem, got_sem, self_sem, fwd_sem, fgot_sem, cput_sem, cgot_sem,
     rput_sem, rgot_sem, zput_sem, zgot_sem, hput_sem, hgot_sem, hself_sem,
@@ -105,10 +105,10 @@
         wide = jnp.where(image == wanted, mm(scores, spread), 0.0).astype(BF)
         return tn(wide, values).astype(BF).reshape(64, 2, 2, values.shape[1])
 
-    def put(t, expert, hidden, slot, group):
+    def put(t, expert, hidden, slot, piece):
         return pltpu.make_async_remote_copy(
             src_ref=send.at[t, expert], dst_ref=rows[t].at[c, slot],
-            send_sem=put_sem.at[t], recv_sem=got_sem.at[t, group],
+            send_sem=put_sem.at[t], recv_sem=got_sem.at[t, piece],
             device_id=(expert, hidden), device_id_type=MESH,
         )
 
@@ -119,20 +119,21 @@
     def send_all(t):
         def far(b, carry):
             dx, dy = odd_even(b, 1 - zl)
-            put(t, expert_at(dx, dy, 2), 2 * (1 - zl) + c, 16 + 8 * (1 - zl) + b, 1).start()
-            return carry
-
-        def near(i, carry):
-            put(t, expert_at(i // 4, i % 4, 3 - 2 * zl), 2 * (1 - zl) + c, 32 * (1 - zl) + i, 0).start()
+            put(t, expert_at(dx, dy, 2), 2 * (1 - zl) + c, 16 + 8 * (1 - zl) + b, 0).start()
+            return carry
+
+        def near(piece, i, carry):
+            put(t, expert_at(i // 4, i % 4, 3 - 2 * zl), 2 * (1 - zl) + c, 32 * (1 - zl) + i, piece).start()
             return carry
 
         def level(i, carry):
-            put(t, expert_at(i // 4, i % 4, 0), h, 48 + i, 2).start()
+            put(t, expert_at(i // 4, i % 4, 0), h, 48 + i, 3).start()
             return carry
 
         pltpu.make_async_copy(send.at[t, e], rows[t].at[c, 48], self_sem.at[t]).start()
         lax.fori_loop(0, 8, far, 0)
-        lax.fori_loop(0, 16, near, 0)
+        lax.fori_loop(0, 8, functools.partial(near, 1), 0)
+        lax.fori_loop(8, 16, functools.partial(near, 2), 0)
         lax.fori_loop(1, 16, level, 0)
 
     def wait_for(ref, sem):
@@ -156,89 +157,97 @@
 
     pair = (e, 2 * (1 - zl) + c)
     mate = (e, 2 * zl + 1 - c)
-    base_a = 32 * zl
-    base_b = 16 + 8 * zl
-    pair_a = 32 * (1 - zl)
-    pair_b = 16 + 8 * (1 - zl)
-
-    def share(t, which, start, count):
-        piece = rows[t].at[c, pl.ds(start, count)]
+    starts = (
+        16 + 8 * zl, 32 * zl, 32 * zl + 8, 48,
+        16 + 8 * (1 - zl), 32 * (1 - zl), 32 * (1 - zl) + 8,
+    )
+    counts = (8, 8, 8, 16, 8, 8, 8)
+
+    def piece_ref(t, i):
+        return rows[t].at[c, pl.ds(starts[i], counts[i])]
+
+    def share(t, i):
         pltpu.make_async_remote_copy(
-            src_ref=piece, dst_ref=piece, send_sem=cput_sem.at[t, which], recv_sem=cgot_sem.at[t, which],
-            device_id=mate, device_id_type=MESH,
+            src_ref=piece_ref(t, i), dst_ref=piece_ref(t, i), send_sem=cput_sem.at[t, i],
+            recv_sem=cgot_sem.at[t, i], device_id=mate, device_id_type=MESH,
         ).start()
 
-    def forward(t, which, start, count):
-        piece = rows[t].at[c, pl.ds(start, count)]
+    def forward(t, i):
         pltpu.make_async_remote_copy(
-            src_ref=piece, dst_ref=piece, send_sem=fwd_sem.at[t, which], recv_sem=fgot_sem.at[t, which],
-            device_id=pair, device_id_type=MESH,
+            src_ref=piece_ref(t, i), dst_ref=piece_ref(t, i), send_sem=fwd_sem.at[t, i],
+            recv_sem=fgot_sem.at[t, i], device_id=pair, device_id_type=MESH,
         ).start()
 
-    def gather_rows(t):
-        wait_for(rows[t].at[c, pl.ds(base_b, 8)], got_sem.at[t, 1])
-        forward(t, 1, base_b, 8)
-        share(t, 1, base_b, 8)
-        wait_for(rows[t].at[c, pl.ds(base_a, 16)], got_sem.at[t, 0])
-        forward(t, 0, base_a, 16)
-        share(t, 0, base_a, 16)
-        wait_for(rows[t].at[c, pl.ds(49, 15)], got_sem.at[t, 2])
-        pltpu.make_async_copy(send.at[t, e], rows[t].at[c, 48], self_sem.at[t]).wait()
-        share(t, 2, 48, 16)
-        wait_for(rows[t].at[c, pl.ds(pair_b, 8)], fgot_sem.at[t, 1])
-        share(t, 3, pair_b, 8)
-        wait_for(rows[t].at[c, pl.ds(pair_a, 16)], fgot_sem.at[t, 0])
-        share(t, 4, pair_a, 16)
-        wait_for(rows[t].at[c, pl.ds(0, 8)], cgot_sem.at[t, 1])
-        wait_for(rows[t].at[c, pl.ds(0, 16)], cgot_sem.at[t, 0])
-        wait_for(rows[t].at[c, pl.ds(0, 16)], cgot_sem.at[t, 2])
-        wait_for(rows[t].at[c, pl.ds(0, 8)], cgot_sem.at[t, 3])
-        wait_for(rows[t].at[c, pl.ds(0, 16)], cgot_sem.at[t, 4])
+    def take(t, i):
+        if i == 3:
+            wait_for(rows[t].at[c, pl.ds(49, 15)], got_sem.at[t, 3])
+            pltpu.make_async_copy(send.at[t, e], rows[t].at[c, 48], self_sem.at[t]).wait()
+        elif i < 3:
+            wait_for(piece_ref(t, i), got_sem.at[t, i])
+            forward(t, i)
+        else:
+            wait_for(piece_ref(t, i), fgot_sem.at[t, i - 4])
+        share(t, i)
+
+    def complete(t):
+        for i, count in enumerate(counts):
+            wait_for(rows[t].at[c, pl.ds(0, count)], cgot_sem.at[t, i])
 
     width = tok4.shape[2]
 
     def expert_rows(t, k):
         return rows[t][:, :, k].reshape(256, width)
 
-    def core_copy(t):
+    def gone(k):
+        return (
+            (pl.ds(16, 16), pl.ds(zl, 1)), (pl.ds(32 * (1 - zl), 8), pl.ds(0, 2)),
+            (pl.ds(32 * (1 - zl) + 8, 8), pl.ds(0, 2)), (pl.ds(48, 16), pl.ds(1 - zl, 1)),
+        )[k]
+
+    def kept(k):
+        return (
+            (pl.ds(16, 16), pl.ds(1 - zl, 1)), (pl.ds(32 * zl, 8), pl.ds(0, 2)),
+            (pl.ds(32 * zl + 8, 8), pl.ds(0, 2)), (pl.ds(48, 16), pl.ds(zl, 1)),
+        )[k]
+
+    landing = (
+        (pl.ds(16, 16), pl.ds(0, 1)), (pl.ds(0, 8), pl.ds(0, 2)),
+        (pl.ds(8, 8), pl.ds(0, 2)), (pl.ds(16, 16), pl.ds(1, 1)),
+    )
+
+    def to_core(t):
+        for half, pieces in enumerate((gone, kept)):
+            for k in range(4):
+                s, j = pieces(k)
+                pltpu.make_async_remote_copy(
+                    src_ref=part.at[t, 1 - c, s, j], dst_ref=fromcore.at[t, s, j], send_sem=rput_sem.at[t],
+                    recv_sem=rgot_sem.at[t, half], device_id=mate, device_id_type=MESH,
+                ).start()
+
+    def add_core(t, half):
+        wait_for(fromcore.at[t, pl.ds(0, 32)], rgot_sem.at[t, half])
+        for k in range(4):
+            s, j = (gone, kept)[half](k)
+            part[t, c, s, j] = (part[t, c, s, j].astype(F32) + fromcore[t, s, j].astype(F32)).astype(BF)
+
+    def to_pair(t, k):
+        s, j = gone(k)
+        ls, lj = landing[k]
         return pltpu.make_async_remote_copy(
-            src_ref=part.at[t, 1 - c], dst_ref=fromcore.at[t], send_sem=rput_sem.at[t], recv_sem=rgot_sem.at[t],
-            device_id=mate, device_id_type=MESH,
+            src_ref=part.at[t, c, s, j], dst_ref=frompair.at[t, ls, lj], send_sem=zput_sem.at[t, k],
+            recv_sem=zgot_sem.at[t, k], device_id=pair, device_id_type=MESH,
         )
 
-    def pair_copies(t):
-        sent = (
-            part.at[t, c, pl.ds(32 * (1 - zl), 16)],
-            part.at[t, c, pl.ds(16, 16), pl.ds(zl, 1)],
-            part.at[t, c, pl.ds(48, 16), pl.ds(1 - zl, 1)],
-        )
-        land = (
-            frompair.at[t, pl.ds(0, 16)],
-            frompair.at[t, pl.ds(16, 16), pl.ds(0, 1)],
-            frompair.at[t, pl.ds(16, 16), pl.ds(1, 1)],
-        )
-        return [
-            pltpu.make_async_remote_copy(
-                src_ref=s, dst_ref=d, send_sem=zput_sem.at[t, i], recv_sem=zgot_sem.at[t, i],
-                device_id=pair, device_id_type=MESH,
-            )
-            for i, (s, d) in enumerate(zip(sent, land))
-        ]
-
-    def add_core(t):
-        core_copy(t).wait_recv()
-        mine = part[t, c]
-        part[t, c] = (mine.astype(F32) + fromcore[t].astype(F32)).astype(BF)
-
-    def add_pair(t):
-        for copy in pair_copies(t):
-            copy.wait_recv()
-        first = part[t, c, pl.ds(32 * zl, 16)].astype(F32)
-        frompair[t, 0:16] = (frompair[t, 0:16].astype(F32) + first).astype(BF)
-        second = part[t, c, 16:32, pl.ds(1 - zl, 1)].astype(F32)
-        frompair[t, 16:32, 0:1] = (frompair[t, 16:32, 0:1].astype(F32) + second).astype(BF)
-        third = part[t, c, 48:64, pl.ds(zl, 1)].astype(F32)
-        frompair[t, 16:32, 1:2] = (frompair[t, 16:32, 1:2].astype(F32) + third).astype(BF)
+    def pair_up(t):
+        add_core(t, 0)
+        for k in range(4):
+            to_pair(t, k).start()
+
+    def add_pair(t, k):
+        to_pair(t, k).wait_recv()
+        s, j = kept(k)
+        ls, lj = landing[k]
+        frompair[t, ls, lj] = (frompair[t, ls, lj].astype(F32) + part[t, c, s, j].astype(F32)).astype(BF)
 
     def go_home(t):
         def put_home(slot, j, expert, hidden):
@@ -263,43 +272,59 @@
             put_home(16 + i, 1, expert_at(4 - i // 4, 4 - i % 4, 0), h)
             return carry
 
+        add_pair(t, 0)
+        lax.fori_loop(0, 8, far, 0)
+        add_pair(t, 1)
+        lax.fori_loop(0, 8, near, 0)
+        add_pair(t, 2)
+        lax.fori_loop(8, 16, near, 0)
+        add_pair(t, 3)
         pltpu.make_async_copy(frompair.at[t, 16, 1], home.at[t, e], hself_sem.at[t]).start()
-        lax.fori_loop(0, 8, far, 0)
-        lax.fori_loop(0, 16, near, 0)
         lax.fori_loop(1, 16, level, 0)
 
-    def interleave(k, product):
-        for n in range(width // 128):
-            inter[n, pl.ds(k, 256, 2), :] = product[:, 128 * n : 128 * n + 128]
-
-    def pack(t):
+    def project(t, cc, product):
+        for k in range(2):
+            rows_k = product(k, act[k, pl.ds(pl.multiple_of(128 * cc, 128), 128)])
+            for n in range(width // 128):
+                inter[n, pl.ds(k, 128, 2), :] = rows_k[:, 128 * n : 128 * n + 128]
         both = jnp.concatenate([inter[n] for n in range(width // 128)], axis=1)
-        part[t] = both.astype(BF).reshape(2, n_slots, 2, 2, width)
-
-    gather_rows(0)
+        part[t, cc] = both.astype(BF).reshape(n_slots, 2, 2, width)
+
+    def reduce_first(t, product):
+        project(t, 1 - c, product)
+        to_core(t)
+        project(t, c, product)
+
+    take(0, 0)
+    take(0, 1)
+    take(0, 2)
+    take(0, 3)
+    take(0, 4)
+    take(1, 0)
+    take(0, 5)
+    take(1, 1)
+    take(0, 6)
+    take(1, 2)
+    take(1, 3)
+    complete(0)
     for k in range(2):
         pre = mm(expert_rows(0, k), win[k]) + bin_[k : k + 1]
         half = 0.5 * (1.0 + lax.erf(pre * 0.7071067811865476))
         slope[k] = half + pre * jnp.exp(-0.5 * pre * pre) * 0.3989422804014327
-        interleave(k, mm((pre * half).astype(BF), wout[k]))
-    pack(0)
-    core_copy(0).start()
-    add_core(0)
-    for copy in pair_copies(0):
-        copy.start()
-
-    gather_rows(1)
-    add_pair(0)
+        act[k] = (pre * half).astype(BF)
+    reduce_first(0, lambda k, a: mm(a, wout[k]))
+    pair_up(0)
+    take(1, 4)
+    take(1, 5)
+    take(1, 6)
+    add_core(0, 1)
+    complete(1)
+    for k in range(2):
+        act[k] = (nt(expert_rows(1, k), wout[k]) * slope[k]).astype(BF)
+    reduce_first(1, lambda k, a: nt(a, win[k]))
     go_home(0)
-    for k in range(2):
-        pre_grad = (nt(expert_rows(1, k), wout[k]) * slope[k]).astype(BF)
-        interleave(k, nt(pre_grad, win[k]))
-    pack(1)
-    core_copy(1).start()
-    add_core(1)
-    for copy in pair_copies(1):
-        copy.start()
-    add_pair(1)
+    pair_up(1)
+    add_core(1, 1)
     go_home(1)
 
     def wait_home(t):
@@ -321,13 +346,13 @@
 
     for t in range(2):
         wait_for(send.at[t, pl.ds(0, 39)], put_sem.at[t])
-        wait_for(rows[t].at[0, pl.ds(0, 16)], fwd_sem.at[t, 0])
-        wait_for(rows[t].at[0, pl.ds(0, 8)], fwd_sem.at[t, 1])
-        for which, count in enumerate((16, 8, 16, 8, 16)):
-            wait_for(rows[t].at[0, pl.ds(0, count)], cput_sem.at[t, which])
-        core_copy(t).wait_send()
-        for copy in pair_copies(t):
-            copy.wait_send()
+        for i in range(3):
+            wait_for(rows[t].at[0, pl.ds(0, 8)], fwd_sem.at[t, i])
+        for i, count in enumerate(counts):
+            wait_for(rows[t].at[0, pl.ds(0, count)], cput_sem.at[t, i])
+        wait_for(fromcore.at[t], rput_sem.at[t])
+        for k in range(4):
+            to_pair(t, k).wait_send()
         wait_for(home.at[t, pl.ds(0, 63)], hput_sem.at[t])
 
 
@@ -356,7 +381,8 @@
             pltpu.VMEM((2, 64, 2, 2, width), BF),
             pltpu.VMEM((2, 64, 2, 2, width), BF),
             pltpu.VMEM((2, 256, units), F32),
-            pltpu.VMEM((width // 128, 512, 128), F32),
+            pltpu.VMEM((2, 256, units), BF),
+            pltpu.VMEM((width // 128, 256, 128), F32),
             pltpu.VMEM((2, 2, 64, 2, 2, width), BF),
             pltpu.VMEM((2, 64, 2, 2, width), BF),
             pltpu.VMEM((2, 32, 2, 2, width), BF),
@@ -366,8 +392,8 @@
             pltpu.VMEM((positions, slots), F32),
             pltpu.VMEM((positions, slots), F32),
             pltpu.VMEM((positions * images, slots), BF),
-            dma((7,)), dma((2,)), dma((2, 3)), dma((2,)), dma((2, 2)), dma((2, 2)), dma((2, 5)), dma((2, 5)),
-            dma((2,)), dma((2,)), dma((2, 3)), dma((2, 3)), dma((2,)), dma((2,)), dma((2,)),
+            dma((7,)), dma((2,)), dma((2, 4)), dma((2,)), dma((2, 3)), dma((2, 3)), dma((2, 7)), dma((2, 7)),
+            dma((2,)), dma((2, 2)), dma((2, 4)), dma((2, 4)), dma((2,)), dma((2,)), dma((2,)),
         ],
         compiler_params=pltpu.CompilerParams(
             collective_id=0, has_side_effects=True, vmem_limit_bytes=58 * 1024 * 1024

time: 71.6 us -> 60.7 us (0.85)
  Pallas kernels: 69.7 us -> 58.8 us
    pallas_call x1, Pallas kernels: 69.7 us -> 58.8 us  [local(): pl.pallas_call(kernel, out_shape=jax.ShapeDtypeStruct((positions, width),...]
where the time goes in v2:
time: 60.7 us; the launch traced here: 60.6 us
  Pallas kernels  58.8 us (97%)
  local copies, waits for them, and re-layouts  1.78 us (3%)
    pallas_call x1, Pallas kernels, local(): pl.pallas_call(kernel, out_shape=jax.ShapeDtypeStruct((positions, width),...  58.8 us
    unnamed x1, local copies, waits for them, and re-layouts  1.78 us

profile of v2, /device:TPU:1, one launch (start us, length us, event | category | flops | bytes accessed | tf_op | source)
XLA Modules:
  0.0 60.6 jit_solution(11569743101436760916)
XLA Ops:
  0.0 58.8 %moe_input_grad.1 = bf16[196,1024]{1,0:T(8,128)(2,1)} custom-call(bf16[196,4,1024]{2,1,0:T(4,128)(2,1)} %bitcast.4, bf16[196,4,1024]{2,1,0:T(4,128)(2,1)} %bitcast.5, bf16[1024,128]{1,0:T(8,128)(2,1)} %keys_h.1, bf16[2,1024,1024]{2,1,0:T(8,128)(2,1)} %win_h.1, f32[2,1024]{1,0:T(2,128)} %bin_h.1, bf16[2,1024,1024]{2,1,0:T(8,128)(2,1)} %wout_h.1, ...), custom_call_target="tpu_custom_call" | custom-call | tf_op jit(solution)/shard_map/moe_input_grad/pallas_call | solution.py:365
  58.8 1.8 %copy.9 = bf16[1,196,1024]{2,1,0:T(8,128)(2,1)} copy(bf16[1,196,1024]{2,1,0:T(8,128)(2,1)} %bitcast.3) | data formatting | bytes 802816

commit v3 on v2

v3 whole, which is shorter than its diff:
```python
import functools

import jax
import jax.numpy as jnp
from jax import lax
from jax.experimental import pallas as pl
from jax.experimental.pallas import tpu as pltpu
from jax.sharding import PartitionSpec as P

BF = jnp.bfloat16
F32 = jnp.float32
MESH = pl.DeviceIdType.MESH
NT = (((1,), (1,)), ((), ()))
TN = (((0,), (0,)), ((), ()))


def mm(a, b):
    return jnp.dot(a, b, preferred_element_type=F32)


def nt(a, b):
    return lax.dot_general(a, b, NT, preferred_element_type=F32)


def tn(a, b):
    return lax.dot_general(a, b, TN, preferred_element_type=F32)


def onehot(shape, test):
    rows = lax.broadcasted_iota(jnp.int32, shape, 0)
    cols = lax.broadcasted_iota(jnp.int32, shape, 1)
    return jnp.where(test(rows, cols), 1.0, 0.0)


def kernel(
    tok_h, grad_h, keys_h, win_h, bin_h, wout_h, bout_h,
    out_ref,
    tok4, grad4, tok, grad, keys, win, wout, bin_, bout,
    send, rows0, rows1, slope, act, inter, part, fromcore, frompair, home,
    own_tok, own_grad, own_disp, own_comb, comb_all, disp_all, scores, flipped,
    load_sem, put_sem, got_sem, self_sem, fwd_sem, fgot_sem, cput_sem, cgot_sem,
    rput_sem, rgot_sem, zput_sem, zgot_sem, hput_sem, hgot_sem, hself_sem,
):
    e = lax.axis_index("expert")
    h = lax.axis_index("hidden")
    x, y, p = e // 16, (e // 4) % 4, e % 4
    zl, c = h // 2, h % 2
    n_slots, positions = 64, tok4.shape[0]
    rows_all = positions * 4
    rows = (rows0, rows1)

    xs = [lax.rem(x + d, 4) * 16 for d in range(4)]
    ys = [lax.rem(y + d, 4) * 4 for d in range(4)]
    ps = [lax.rem(p + d, 4) for d in range(4)]
    ahead = lax.rem(p + 3 - 2 * zl, 4)
    offsets = (
        (0, 0), (1, 0), (0, 1), (3, 0), (0, 3), (1, 1), (3, 3), (1, 3),
        (3, 1), (2, 0), (0, 2), (2, 1), (1, 2), (2, 3), (3, 2), (2, 2),
    )

    def expert_at(dx, dy, plane):
        return xs[dx % 4] + ys[dy % 4] + plane

    def checkered(flip):
        return [(b // 2, 2 * (b % 2) + (b // 2 + flip) % 2) for b in range(8)]

    swapped = [lax.rem(y + d, 4) * 4 for d in (1 - zl, zl, 3 - zl, 2 + zl)]

    loads = [
        pltpu.make_async_copy(src, dst, load_sem.at[i])
        for i, (src, dst) in enumerate((
            (tok_h, tok4), (keys_h, keys), (grad_h, grad4), (win_h, win), (bin_h, bin_),
            (wout_h, wout), (bout_h, bout),
        ))
    ]
    loads[0].start()
    loads[1].start()

    barrier = pltpu.get_barrier_semaphore()

    def greet(expert, hidden):
        pl.semaphore_signal(barrier, inc=1, device_id=(expert, hidden), device_id_type=MESH)

    for dx, dy in offsets[::-1]:
        greet(expert_at(dx, dy, ps[2]), 2 * (1 - zl) + c)
        greet(expert_at(dx, dy, ps[1]), c)
        greet(expert_at(dx, dy, ps[3]), 2 + c)
    for dx, dy in offsets[:0:-1]:
        greet(expert_at(dx, dy, ps[0]), h)
    greet(e, 2 * (1 - zl) + c)
    greet(e, 2 * zl + 1 - c)
    for copy in loads[2:]:
        copy.start()

    loads[0].wait()
    loads[1].wait()
    tok[...] = tok4[...].reshape(rows_all, tok4.shape[2])
    logits = mm(tok[...], keys[...])
    folded = logits.reshape(rows_all // 8, 8, logits.shape[1])
    top = jnp.max(folded, axis=0)
    top = jnp.maximum(top, pltpu.roll(top, 4, 0))
    weight = jnp.exp(folded - top[None])
    total = jnp.sum(weight, axis=0)
    total = total + pltpu.roll(total, 4, 0)
    dispatch = (weight / total[None]).reshape(rows_all, logits.shape[1]).astype(BF)
    disp_all[...] = dispatch
    scores[...] = logits
    spread = onehot((128, 256), lambda r, q: q // 2 == r).astype(BF)
    image = lax.broadcasted_iota(jnp.int32, (rows_all, 256), 0) % 4
    wanted = c + 2 * (lax.broadcasted_iota(jnp.int32, (rows_all, 256), 1) % 2)

    def slots(scores, values):
        wide = jnp.where(image == wanted, mm(scores, spread), 0.0).astype(BF)
        return tn(wide, values).astype(BF).reshape(64, 2, 2, values.shape[1])

    def put(t, expert, hidden, slot, piece):
        return pltpu.make_async_remote_copy(
            src_ref=send.at[t, expert], dst_ref=rows[t].at[c, slot],
            send_sem=put_sem.at[t], recv_sem=got_sem.at[t, piece],
            device_id=(expert, hidden), device_id_type=MESH,
        )

    def send_all(t):
        def far(b):
            dx = b // 2
            expert = xs[dx] + swapped[2 * (b % 2) + dx % 2] + ps[2]
            put(t, expert, 2 * (1 - zl) + c, 16 + 8 * (1 - zl) + b, 0).start()

        def near(i):
            put(t, expert_at(*offsets[i], ahead), 2 * (1 - zl) + c, 32 * (1 - zl) + i, 1 + i // 4).start()

        def level(i):
            put(t, expert_at(*offsets[i], ps[0]), h, 48 + i, 5).start()

        pltpu.make_async_copy(send.at[t, e], rows[t].at[c, 48], self_sem.at[t]).start()
        for i in range(16):
            near(i)
            if t == 0 and 3 < i < 12:
                far(i - 4)
            if i:
                level((i + 7) % 15 + 1)
        if t == 1:
            for b in range(8):
                far(b)

    def wait_for(ref, sem):
        pltpu.make_async_copy(ref, ref, sem).wait()

    send[0] = slots(dispatch, tok[...])
    pl.semaphore_wait(barrier, 65)
    send_all(0)
    weight = jnp.exp(scores[...] - jnp.max(scores[...], axis=1, keepdims=True))
    comb_all[...] = (weight / jnp.sum(weight, axis=1, keepdims=True)).astype(BF)
    loads[2].wait()
    grad[...] = grad4[...].reshape(rows_all, grad4.shape[2])
    send[1] = slots(comb_all[...], grad[...])
    pair = (e, 2 * (1 - zl) + c)
    mate = (e, 2 * zl + 1 - c)
    starts = (
        16 + 8 * zl, *(32 * zl + 4 * q for q in range(4)), 48,
        16 + 8 * (1 - zl), *(32 * (1 - zl) + 4 * q for q in range(4)),
    )
    counts = (8, *(4,) * 4, 16, 8, *(4,) * 4)

    def piece_ref(t, i):
        return rows[t].at[c, pl.ds(starts[i], counts[i])]

    def share(t, i):
        pltpu.make_async_remote_copy(
            src_ref=piece_ref(t, i), dst_ref=piece_ref(t, i), send_sem=cput_sem.at[t, i],
            recv_sem=cgot_sem.at[t, i], device_id=mate, device_id_type=MESH,
        ).start()

    def forward(t, i):
        pltpu.make_async_remote_copy(
            src_ref=piece_ref(t, i), dst_ref=piece_ref(t, i), send_sem=fwd_sem.at[t, i],
            recv_sem=fgot_sem.at[t, i], device_id=pair, device_id_type=MESH,
        ).start()

    def take(t, i):
        if i == 5:
            wait_for(rows[t].at[c, pl.ds(49, 15)], got_sem.at[t, i])
            pltpu.make_async_copy(send.at[t, e], rows[t].at[c, 48], self_sem.at[t]).wait()
        elif i < 5:
            wait_for(piece_ref(t, i), got_sem.at[t, i])
            forward(t, i)
        else:
            wait_for(piece_ref(t, i), fgot_sem.at[t, i - 6])

    def complete(t):
        for i, count in enumerate(counts):
            wait_for(rows[t].at[c, pl.ds(0, count)], cgot_sem.at[t, i])

    width = tok4.shape[2]

    def gone(k):
        return (
            (pl.ds(16, 16), pl.ds(zl, 1)), (pl.ds(32 * (1 - zl) + 8, 8), pl.ds(0, 2)),
            (pl.ds(32 * (1 - zl), 8), pl.ds(0, 2)), (pl.ds(52, 12), pl.ds(1 - zl, 1)), (pl.ds(48, 4), pl.ds(1 - zl, 1)),
        )[k]

    def kept(k):
        return (
            (pl.ds(16, 16), pl.ds(1 - zl, 1)), (pl.ds(32 * zl + 8, 8), pl.ds(0, 2)),
            (pl.ds(32 * zl, 8), pl.ds(0, 2)), (pl.ds(52, 12), pl.ds(zl, 1)), (pl.ds(48, 4), pl.ds(zl, 1)),
        )[k]

    landing = (
        (pl.ds(16, 16), pl.ds(0, 1)), (pl.ds(8, 8), pl.ds(0, 2)),
        (pl.ds(0, 8), pl.ds(0, 2)), (pl.ds(20, 12), pl.ds(1, 1)), (pl.ds(16, 4), pl.ds(1, 1)),
    )

    def to_core(t):
        for half, pieces in enumerate((gone, kept)):
            for k in range(5):
                s, j = pieces(k)
                pltpu.make_async_remote_copy(
                    src_ref=part.at[t, 1 - c, s, j], dst_ref=fromcore.at[t, s, j], send_sem=rput_sem.at[t],
                    recv_sem=rgot_sem.at[t, half], device_id=mate, device_id_type=MESH,
                ).start()

    def add_core(t, half):
        wait_for(fromcore.at[t, pl.ds(0, 32)], rgot_sem.at[t, half])
        for k in range(5):
            s, j = (gone, kept)[half](k)
            part[t, c, s, j] = (part[t, c, s, j].astype(F32) + fromcore[t, s, j].astype(F32)).astype(BF)

    def to_pair(t, k):
        s, j = gone(k)
        ls, lj = landing[k]
        return pltpu.make_async_remote_copy(
            src_ref=part.at[t, c, s, j], dst_ref=frompair.at[t, ls, lj], send_sem=zput_sem.at[t, k],
            recv_sem=zgot_sem.at[t, k], device_id=pair, device_id_type=MESH,
        )

    def pair_up(t):
        add_core(t, 0)
        for k in range(5):
            to_pair(t, k).start()

    def add_pair(t, k):
        to_pair(t, k).wait_recv()
        s, j = kept(k)
        ls, lj = landing[k]
        frompair[t, ls, lj] = (frompair[t, ls, lj].astype(F32) + part[t, c, s, j].astype(F32)).astype(BF)

    def go_home(t, piece):
        def put_home(slot, j, expert, hidden):
            pltpu.make_async_remote_copy(
                src_ref=frompair.at[t, slot, j], dst_ref=home.at[t, e], send_sem=hput_sem.at[t],
                recv_sem=hgot_sem.at[t], device_id=(expert, hidden), device_id_type=MESH,
            ).start()

        def far():
            for par in (0, 1):
                for b, (dx, dy) in enumerate(checkered(par)):
                    put_home(16 + 8 * par + b, 0, expert_at(-dx, -dy, ps[2]), 2 * (1 - zl) + c)

        def near(first, last):
            for i in range(first, last):
                dx, dy = offsets[i]
                expert = expert_at(-dx, -dy, ahead)
                put_home(i, 0, expert, c)
                put_home(i, 1, expert, 2 + c)

        def level(first, last):
            for i in range(first, last):
                dx, dy = offsets[i]
                put_home(16 + i, 1, expert_at(-dx, -dy, ps[0]), h)

        add_pair(t, piece)
        if piece == 0:
            far()
        elif piece == 1:
            near(8, 16)
        elif piece == 2:
            near(0, 8)
        elif piece == 3:
            level(4, 16)
        else:
            pltpu.make_async_copy(frompair.at[t, 16, 1], home.at[t, e], hself_sem.at[t]).start()
            level(1, 4)

    def project(t, cc, weights):
        for k in range(2):
            rows_k = mm(act[k, pl.ds(pl.multiple_of(128 * cc, 128), 128)], weights[k])
            for n in range(width // 128):
                inter[n, pl.ds(k, 128, 2), :] = rows_k[:, 128 * n : 128 * n + 128]
        both = jnp.concatenate([inter[n] for n in range(width // 128)], axis=1)
        part[t, cc] = both.astype(BF).reshape(n_slots, 2, 2, width)


    def take_share(t, *pieces):
        for i in pieces:
            take(t, i)
            share(t, i)

    def take_on(t, *pieces):
        for i in pieces:
            take(t, i)

    def half_rows(t, k, cc):
        return rows[t][cc, :, k].reshape(128, width)

    def gate(k, cc):
        place = pl.ds(pl.multiple_of(128 * cc, 128), 128)
        pre = mm(half_rows(0, k, cc), win[k]) + bin_[k : k + 1]
        half = 0.5 * (1.0 + lax.erf(pre * 0.7071067811865476))
        slope[k, place] = half + pre * jnp.exp(-0.5 * pre * pre) * 0.3989422804014327
        act[k, place] = (pre * half).astype(BF)

    def slopes(cc):
        place = pl.ds(pl.multiple_of(128 * cc, 128), 128)
        for k in range(2):
            act[k, place] = (nt(half_rows(1, k, cc), wout[k]) * slope[k, place]).astype(BF)

    def slopes_all():
        for k in range(2):
            act[k] = (nt(rows[1][:, :, k].reshape(256, width), wout[k]) * slope[k]).astype(BF)

    def landed():
        for copy in loads[3:]:
            copy.wait()

    def flip():
        for k in range(2):
            flipped[k] = win[k].T

    landed()
    flip()
    take_share(0, 1)

    @pl.when(c == 0)
    def _():
        send_all(1)

    take_share(0, 2, 0, 3, 4, 5)

    @pl.when(c == 1)
    def _():
        send_all(1)

    take_share(0, 7, 8, 6, 9, 10)
    gate(0, c)
    gate(1, c)
    complete(0)
    take_on(1, 1, 2)
    gate(0, 1 - c)
    take_on(1, 3)
    gate(1, 1 - c)
    take_on(1, 4, 5)
    project(0, 1 - c, wout)
    to_core(0)
    take_on(1, 0)
    for piece in (1, 2, 3, 4, 5, 0):
        share(1, piece)
    project(0, c, wout)
    pair_up(0)
    take_share(1, 7, 8, 9, 10, 6)
    add_core(0, 1)
    complete(1)
    slopes_all()
    go_home(0, 0)
    project(1, 1 - c, flipped)
    to_core(1)
    go_home(0, 1)
    project(1, c, flipped)
    pair_up(1)
    for piece in range(2, 5):
        go_home(0, piece)
    add_core(1, 1)
    pick = onehot((positions, rows_all), lambda r, q: q == 4 * r + h).astype(BF)
    own_tok[...] = mm(pick, tok[...]).astype(BF)
    own_grad[...] = mm(pick, grad[...]).astype(BF)
    own_disp[...] = mm(pick, disp_all[...])
    own_comb[...] = mm(pick, comb_all[...])
    for piece in range(5):
        go_home(1, piece)

    def wait_home(t):
        wait_for(home.at[t, pl.ds(0, 63)], hgot_sem.at[t])
        pltpu.make_async_copy(frompair.at[t, 16, 1], home.at[t, e], hself_sem.at[t]).wait()

    wait_home(0)
    slot_out = (home[0].reshape(128, width).astype(F32) + bout[...]).astype(BF)
    comb = own_comb[...]
    disp = own_disp[...]
    comb_grad = nt(own_grad[...], slot_out)
    comb_term = comb * (comb_grad - jnp.sum(comb * comb_grad, axis=1, keepdims=True))
    wait_home(1)
    slot_in_grad = home[1].reshape(128, width)
    disp_grad = nt(own_tok[...], slot_in_grad)
    logit_grad = comb_term + disp * (disp_grad - jnp.sum(disp * disp_grad, axis=0, keepdims=True))
    result = mm(disp.astype(BF), slot_in_grad) + nt(logit_grad.astype(BF), keys[...])
    out_ref[...] = result.astype(BF)

    for t in range(2):
        wait_for(send.at[t, pl.ds(0, 39)], put_sem.at[t])
        for i in range(5):
            wait_for(rows[t].at[0, pl.ds(0, counts[i])], fwd_sem.at[t, i])
        for i, count in enumerate(counts):
            wait_for(rows[t].at[0, pl.ds(0, count)], cput_sem.at[t, i])
        wait_for(fromcore.at[t], rput_sem.at[t])
        for k in range(5):
            to_pair(t, k).wait_send()
        wait_for(home.at[t, pl.ds(0, 63)], hput_sem.at[t])


def local(tokens, slot_keys, w_in, b_in, w_out, b_out, out_grad):
    images, positions, width = tokens.shape
    units = w_in.shape[2]
    slots = slot_keys.shape[1]
    anyspec = pl.BlockSpec(memory_space=pl.ANY)
    dma = pltpu.SemaphoreType.DMA
    out = pl.pallas_call(
        kernel,
        out_shape=pltpu.VMEM((positions, width), BF),
        in_specs=[anyspec] * 7,
        out_specs=pl.BlockSpec(memory_space=pltpu.VMEM),
        scratch_shapes=[
            pltpu.VMEM((positions, images, width), BF),
            pltpu.VMEM((positions, images, width), BF),
            pltpu.VMEM((positions * images, width), BF),
            pltpu.VMEM((positions * images, width), BF),
            pltpu.VMEM((width, slots), BF),
            pltpu.VMEM((2, width, units), BF),
            pltpu.VMEM((2, units, width), BF),
            pltpu.VMEM((2, units), F32),
            pltpu.VMEM((slots, width), F32),
            pltpu.VMEM((2, 64, 2, 2, width), BF),
            pltpu.VMEM((2, 64, 2, 2, width), BF),
            pltpu.VMEM((2, 64, 2, 2, width), BF),
            pltpu.VMEM((2, 256, units), F32),
            pltpu.VMEM((2, 256, units), BF),
            pltpu.VMEM((width // 128, 256, 128), F32),
            pltpu.VMEM((2, 2, 64, 2, 2, width), BF),
            pltpu.VMEM((2, 64, 2, 2, width), BF),
            pltpu.VMEM((2, 32, 2, 2, width), BF),
            pltpu.VMEM((2, 64, 2, width), BF),
            pltpu.VMEM((positions, width), BF),
            pltpu.VMEM((positions, width), BF),
            pltpu.VMEM((positions, slots), F32),
            pltpu.VMEM((positions, slots), F32),
            pltpu.VMEM((positions * images, slots), BF),
            pltpu.VMEM((positions * images, slots), BF),
            pltpu.VMEM((positions * images, slots), F32),
            pltpu.VMEM((2, units, width), BF),
            dma((7,)), dma((2,)), dma((2, 6)), dma((2,)), dma((2, 5)), dma((2, 5)), dma((2, 11)), dma((2, 11)),
            dma((2,)), dma((2, 2)), dma((2, 5)), dma((2, 5)), dma((2,)), dma((2,)), dma((2,)),
        ],
        compiler_params=pltpu.CompilerParams(
            collective_id=0, has_side_effects=True, vmem_limit_bytes=58 * 1024 * 1024
        ),
        name="moe_input_grad",
    )(
        jnp.transpose(tokens, (1, 0, 2)), jnp.transpose(out_grad, (1, 0, 2)), slot_keys, w_in, b_in, w_out, b_out
    )
    return out[None]


def solution(mesh):
    return jax.shard_map(
        local,
        mesh=mesh,
        in_specs=(
            P("expert", None, None),
            P(),
            P("expert", None, "hidden"),
            P("expert", "hidden"),
            P("expert", "hidden", None),
            P(),
            P("expert", None, None),
        ),
        out_specs=P(("expert", "hidden"), None, None),
        check_vma=False,
    )
```

time: 60.7 us -> 56.3 us (0.928)
  Pallas kernels: 58.8 us -> 55.5 us
  local copies, waits for them, and re-layouts: 1.78 us -> 0.75 us
    pallas_call x1, Pallas kernels: 58.8 us -> 55.5 us  [local(): pl.pallas_call(kernel, out_shape=pltpu.VMEM((positions, width), BF), in_s...]
    unnamed x1, local copies, waits for them, and re-layouts: 1.78 us -> 0.75 us
where the time goes in v3:
time: 56.3 us
  Pallas kernels  55.5 us (99%)
  local copies, waits for them, and re-layouts  0.75 us (1%)
    pallas_call x1, Pallas kernels, local(): pl.pallas_call(kernel, out_shape=pltpu.VMEM((positions, width), BF), in_s...  55.5 us

profile of v3, /device:TPU:1, one launch (start us, length us, event | category | flops | bytes accessed | tf_op | source)
XLA Modules:
  0.0 56.3 jit_solution(13839727124947052859)
XLA Ops:
  0.0 55.5 %moe_input_grad.1 = bf16[196,1024]{1,0:T(8,128)(2,1)S(1)} custom-call(bf16[196,4,1024]{2,1,0:T(4,128)(2,1)} %bitcast.4, bf16[196,4,1024]{2,1,0:T(4,128)(2,1)} %bitcast.5, bf16[1024,128]{1,0:T(8,128)(2,1)} %keys_h.1, bf16[2,1024,1024]{2,1,0:T(8,128)(2,1)} %win_h.1, f32[2,1024]{1,0:T(2,128)} %bin_h.1, bf16[2,1024,1024]{2,1,0:T(8,128)(2,1)} %wout_h.1, ...), custom_call_target="tpu_custom_call" | custom-call | tf_op jit(solution)/shard_map/moe_input_grad/pallas_call | solution.py:415
  55.5 0.8 %copy.9 = bf16[1,196,1024]{2,1,0:T(8,128)(2,1)} copy(bf16[1,196,1024]{2,1,0:T(8,128)(2,1)S(1)} %bitcast.3) | data formatting | bytes 802816

commit v4 on v3

--- a/solution.py
+++ b/solution.py
@@ -37,7 +37,7 @@
     out_ref,
     tok4, grad4, tok, grad, keys, win, wout, bin_, bout,
     send, rows0, rows1, slope, act, inter, part, fromcore, frompair, home,
-    own_tok, own_grad, own_disp, own_comb, comb_all, disp_all, scores, flipped,
+    own_tok, own_grad, own_disp, own_comb, comb_all, disp_all, scores, flipped, flipped_out,
     load_sem, put_sem, got_sem, self_sem, fwd_sem, fgot_sem, cput_sem, cgot_sem,
     rput_sem, rgot_sem, zput_sem, zgot_sem, hput_sem, hgot_sem, hself_sem,
 ):
@@ -120,35 +120,26 @@
             device_id=(expert, hidden), device_id_type=MESH,
         )
 
-    def send_all(t):
-        def far(b):
-            dx = b // 2
-            expert = xs[dx] + swapped[2 * (b % 2) + dx % 2] + ps[2]
-            put(t, expert, 2 * (1 - zl) + c, 16 + 8 * (1 - zl) + b, 0).start()
-
-        def near(i):
-            put(t, expert_at(*offsets[i], ahead), 2 * (1 - zl) + c, 32 * (1 - zl) + i, 1 + i // 4).start()
-
-        def level(i):
-            put(t, expert_at(*offsets[i], ps[0]), h, 48 + i, 5).start()
-
+    def send_near(t):
+        for i in range(16):
+            expert = expert_at(*offsets[i], ahead)
+            put(t, expert, 2 * (1 - zl) + c, 16 * (1 - zl) + i, i // 8).start()
+
+    def send_rest(t):
         pltpu.make_async_copy(send.at[t, e], rows[t].at[c, 48], self_sem.at[t]).start()
-        for i in range(16):
-            near(i)
-            if t == 0 and 3 < i < 12:
-                far(i - 4)
-            if i:
-                level((i + 7) % 15 + 1)
-        if t == 1:
-            for b in range(8):
-                far(b)
+        for i in range(1, 16):
+            if i <= 8:
+                b = i - 1
+                expert = xs[b // 2] + swapped[2 * (b % 2) + (b // 2) % 2] + ps[2]
+                put(t, expert, 2 * (1 - zl) + c, 32 + 8 * (1 - zl) + b, 2).start()
+            put(t, expert_at(*offsets[i], ps[0]), h, 48 + i, 3).start()
 
     def wait_for(ref, sem):
         pltpu.make_async_copy(ref, ref, sem).wait()
 
     send[0] = slots(dispatch, tok[...])
     pl.semaphore_wait(barrier, 65)
-    send_all(0)
+    send_near(0)
     weight = jnp.exp(scores[...] - jnp.max(scores[...], axis=1, keepdims=True))
     comb_all[...] = (weight / jnp.sum(weight, axis=1, keepdims=True)).astype(BF)
     loads[2].wait()
@@ -157,71 +148,75 @@
     pair = (e, 2 * (1 - zl) + c)
     mate = (e, 2 * zl + 1 - c)
     starts = (
-        16 + 8 * zl, *(32 * zl + 4 * q for q in range(4)), 48,
-        16 + 8 * (1 - zl), *(32 * (1 - zl) + 4 * q for q in range(4)),
+        16 * zl, 16 * zl + 8, 32 + 8 * zl, 48, 16 * (1 - zl), 16 * (1 - zl) + 8, 32 + 8 * (1 - zl),
     )
-    counts = (8, *(4,) * 4, 16, 8, *(4,) * 4)
+    counts = (8, 8, 8, 16, 8, 8, 8)
 
     def piece_ref(t, i):
         return rows[t].at[c, pl.ds(starts[i], counts[i])]
 
     def share(t, i):
         pltpu.make_async_remote_copy(
-            src_ref=piece_ref(t, i), dst_ref=piece_ref(t, i), send_sem=cput_sem.at[t, i],
-            recv_sem=cgot_sem.at[t, i], device_id=mate, device_id_type=MESH,
+            src_ref=piece_ref(t, i), dst_ref=piece_ref(t, i), send_sem=cput_sem.at[t],
+            recv_sem=cgot_sem.at[t, int(i in (2, 3, 6))], device_id=mate, device_id_type=MESH,
         ).start()
 
     def forward(t, i):
         pltpu.make_async_remote_copy(
-            src_ref=piece_ref(t, i), dst_ref=piece_ref(t, i), send_sem=fwd_sem.at[t, i],
+            src_ref=piece_ref(t, i), dst_ref=piece_ref(t, i), send_sem=fwd_sem.at[t],
             recv_sem=fgot_sem.at[t, i], device_id=pair, device_id_type=MESH,
         ).start()
 
-    def take(t, i):
-        if i == 5:
-            wait_for(rows[t].at[c, pl.ds(49, 15)], got_sem.at[t, i])
-            pltpu.make_async_copy(send.at[t, e], rows[t].at[c, 48], self_sem.at[t]).wait()
-        elif i < 5:
-            wait_for(piece_ref(t, i), got_sem.at[t, i])
-            forward(t, i)
-        else:
-            wait_for(piece_ref(t, i), fgot_sem.at[t, i - 6])
-
-    def complete(t):
-        for i, count in enumerate(counts):
-            wait_for(rows[t].at[c, pl.ds(0, count)], cgot_sem.at[t, i])
+    def take(t, *pieces):
+        for i in pieces:
+            if i == 3:
+                wait_for(rows[t].at[c, pl.ds(49, 15)], got_sem.at[t, i])
+                pltpu.make_async_copy(send.at[t, e], rows[t].at[c, 48], self_sem.at[t]).wait()
+            elif i < 3:
+                wait_for(piece_ref(t, i), got_sem.at[t, i])
+                forward(t, i)
+            else:
+                wait_for(piece_ref(t, i), fgot_sem.at[t, i - 4])
+
+    def share_all(t, *pieces):
+        for i in pieces:
+            share(t, i)
+
+    def complete(t, part_of):
+        wait_for(rows[t].at[c, pl.ds(0, 32)], cgot_sem.at[t, part_of])
 
     width = tok4.shape[2]
 
     def gone(k):
         return (
-            (pl.ds(16, 16), pl.ds(zl, 1)), (pl.ds(32 * (1 - zl) + 8, 8), pl.ds(0, 2)),
-            (pl.ds(32 * (1 - zl), 8), pl.ds(0, 2)), (pl.ds(52, 12), pl.ds(1 - zl, 1)), (pl.ds(48, 4), pl.ds(1 - zl, 1)),
+            (pl.ds(16 * (1 - zl) + 8, 8), pl.ds(0, 2)), (pl.ds(16 * (1 - zl), 8), pl.ds(0, 2)),
+            (pl.ds(32, 16), pl.ds(zl, 1)), (pl.ds(52, 12), pl.ds(1 - zl, 1)), (pl.ds(48, 4), pl.ds(1 - zl, 1)),
         )[k]
 
     def kept(k):
         return (
-            (pl.ds(16, 16), pl.ds(1 - zl, 1)), (pl.ds(32 * zl + 8, 8), pl.ds(0, 2)),
-            (pl.ds(32 * zl, 8), pl.ds(0, 2)), (pl.ds(52, 12), pl.ds(zl, 1)), (pl.ds(48, 4), pl.ds(zl, 1)),
+            (pl.ds(16 * zl + 8, 8), pl.ds(0, 2)), (pl.ds(16 * zl, 8), pl.ds(0, 2)),
+            (pl.ds(32, 16), pl.ds(1 - zl, 1)), (pl.ds(52, 12), pl.ds(zl, 1)), (pl.ds(48, 4), pl.ds(zl, 1)),
         )[k]
 
     landing = (
-        (pl.ds(16, 16), pl.ds(0, 1)), (pl.ds(8, 8), pl.ds(0, 2)),
-        (pl.ds(0, 8), pl.ds(0, 2)), (pl.ds(20, 12), pl.ds(1, 1)), (pl.ds(16, 4), pl.ds(1, 1)),
+        (pl.ds(8, 8), pl.ds(0, 2)), (pl.ds(0, 8), pl.ds(0, 2)),
+        (pl.ds(16, 16), pl.ds(0, 1)), (pl.ds(20, 12), pl.ds(1, 1)), (pl.ds(16, 4), pl.ds(1, 1)),
     )
-
-    def to_core(t):
+    members = ((0, 1), (2, 3, 4))
+
+    def to_core(t, u):
         for half, pieces in enumerate((gone, kept)):
-            for k in range(5):
+            for k in members[u]:
                 s, j = pieces(k)
                 pltpu.make_async_remote_copy(
                     src_ref=part.at[t, 1 - c, s, j], dst_ref=fromcore.at[t, s, j], send_sem=rput_sem.at[t],
-                    recv_sem=rgot_sem.at[t, half], device_id=mate, device_id_type=MESH,
+                    recv_sem=rgot_sem.at[t, 2 * u + half], device_id=mate, device_id_type=MESH,
                 ).start()
 
-    def add_core(t, half):
-        wait_for(fromcore.at[t, pl.ds(0, 32)], rgot_sem.at[t, half])
-        for k in range(5):
+    def add_core(t, u, half):
+        wait_for(fromcore.at[t, pl.ds(0, 16)], rgot_sem.at[t, 2 * u + half])
+        for k in members[u]:
             s, j = (gone, kept)[half](k)
             part[t, c, s, j] = (part[t, c, s, j].astype(F32) + fromcore[t, s, j].astype(F32)).astype(BF)
 
@@ -229,14 +224,18 @@
         s, j = gone(k)
         ls, lj = landing[k]
         return pltpu.make_async_remote_copy(
-            src_ref=part.at[t, c, s, j], dst_ref=frompair.at[t, ls, lj], send_sem=zput_sem.at[t, k],
+            src_ref=part.at[t, c, s, j], dst_ref=frompair.at[t, ls, lj], send_sem=zput_sem.at[t],
             recv_sem=zgot_sem.at[t, k], device_id=pair, device_id_type=MESH,
         )
 
-    def pair_up(t):
-        add_core(t, 0)
-        for k in range(5):
+    def queue(*pieces):
+        for t, k in pieces:
             to_pair(t, k).start()
+
+    def pair_up(t, u, *more):
+        add_core(t, u, 0)
+        for tt, k in more or [(t, k) for k in members[u]]:
+            to_pair(tt, k).start()
 
     def add_pair(t, k):
         to_pair(t, k).wait_recv()
@@ -270,111 +269,110 @@
 
         add_pair(t, piece)
         if piece == 0:
+            near(8, 16)
+        elif piece == 1:
+            near(0, 8)
+        elif piece == 2:
             far()
-        elif piece == 1:
-            near(8, 16)
-        elif piece == 2:
-            near(0, 8)
         elif piece == 3:
             level(4, 16)
         else:
             pltpu.make_async_copy(frompair.at[t, 16, 1], home.at[t, e], hself_sem.at[t]).start()
             level(1, 4)
 
-    def project(t, cc, weights):
+    def unit_rows(t, k, u):
+        return rows[t][:, 32 * u : 32 * u + 32, k].reshape(128, width)
+
+    def gate(u):
         for k in range(2):
-            rows_k = mm(act[k, pl.ds(pl.multiple_of(128 * cc, 128), 128)], weights[k])
+            pre = mm(unit_rows(0, k, u), win[k]) + bin_[k : k + 1]
+            half = 0.5 * (1.0 + lax.erf(pre * 0.7071067811865476))
+            slope[k] = half + pre * jnp.exp(-0.5 * pre * pre) * 0.3989422804014327
+            act[k] = (pre * half).astype(BF)
+
+    def slopes(u):
+        for k in range(2):
+            act[k] = (mm(unit_rows(1, k, u), flipped_out[k]) * slope[k]).astype(BF)
+
+    def project(t, u, weights):
+        for k in range(2):
+            rows_k = mm(act[k], weights[k])
             for n in range(width // 128):
                 inter[n, pl.ds(k, 128, 2), :] = rows_k[:, 128 * n : 128 * n + 128]
         both = jnp.concatenate([inter[n] for n in range(width // 128)], axis=1)
-        part[t, cc] = both.astype(BF).reshape(n_slots, 2, 2, width)
-
-
-    def take_share(t, *pieces):
-        for i in pieces:
-            take(t, i)
-            share(t, i)
-
-    def take_on(t, *pieces):
-        for i in pieces:
-            take(t, i)
-
-    def half_rows(t, k, cc):
-        return rows[t][cc, :, k].reshape(128, width)
-
-    def gate(k, cc):
-        place = pl.ds(pl.multiple_of(128 * cc, 128), 128)
-        pre = mm(half_rows(0, k, cc), win[k]) + bin_[k : k + 1]
-        half = 0.5 * (1.0 + lax.erf(pre * 0.7071067811865476))
-        slope[k, place] = half + pre * jnp.exp(-0.5 * pre * pre) * 0.3989422804014327
-        act[k, place] = (pre * half).astype(BF)
-
-    def slopes(cc):
-        place = pl.ds(pl.multiple_of(128 * cc, 128), 128)
-        for k in range(2):
-            act[k, place] = (nt(half_rows(1, k, cc), wout[k]) * slope[k, place]).astype(BF)
-
-    def slopes_all():
-        for k in range(2):
-            act[k] = (nt(rows[1][:, :, k].reshape(256, width), wout[k]) * slope[k]).astype(BF)
-
+        part[t, :, 32 * u : 32 * u + 32] = both.astype(BF).reshape(2, 32, 2, 2, width)
+        to_core(t, u)
+
+    def own_image():
+        pick = onehot((positions, rows_all), lambda r, q: q == 4 * r + h).astype(BF)
+        own_tok[...] = mm(pick, tok[...]).astype(BF)
+        own_grad[...] = mm(pick, grad[...]).astype(BF)
+        own_disp[...] = mm(pick, disp_all[...])
+        own_comb[...] = mm(pick, comb_all[...])
     def landed():
         for copy in loads[3:]:
             copy.wait()
 
-    def flip():
-        for k in range(2):
-            flipped[k] = win[k].T
-
+    def flip(k):
+        flipped[k] = win[k].T
+        flipped_out[k] = wout[k].T
+
+    send_near(1)
+    send_rest(0)
     landed()
-    flip()
-    take_share(0, 1)
-
-    @pl.when(c == 0)
-    def _():
-        send_all(1)
-
-    take_share(0, 2, 0, 3, 4, 5)
-
-    @pl.when(c == 1)
-    def _():
-        send_all(1)
-
-    take_share(0, 7, 8, 6, 9, 10)
-    gate(0, c)
-    gate(1, c)
-    complete(0)
-    take_on(1, 1, 2)
-    gate(0, 1 - c)
-    take_on(1, 3)
-    gate(1, 1 - c)
-    take_on(1, 4, 5)
-    project(0, 1 - c, wout)
-    to_core(0)
-    take_on(1, 0)
-    for piece in (1, 2, 3, 4, 5, 0):
-        share(1, piece)
-    project(0, c, wout)
-    pair_up(0)
-    take_share(1, 7, 8, 9, 10, 6)
-    add_core(0, 1)
-    complete(1)
-    slopes_all()
+    flip(0)
+    take(0, 0)
+    share_all(0, 0)
+    flip(1)
+    take(0, 1)
+    share_all(0, 1)
+    take(1, 0)
+    send_rest(1)
+    own_image()
+    take(1, 1)
+    take(0, 4, 5)
+    share_all(0, 4, 5)
+    take(0, 2)
+    complete(0, 0)
+    gate(0)
+    share_all(1, 0, 1)
+    take(1, 4)
+    share_all(1, 4)
+    project(0, 0, wout)
+    take(1, 5)
+    share_all(1, 5)
+    take(0, 3)
+    share_all(0, 2, 3)
+    pair_up(0, 0)
+    add_core(0, 0, 1)
+    complete(1, 0)
+    slopes(0)
+    take(1, 2)
+    project(1, 0, flipped)
+    take(0, 6)
+    share_all(0, 6)
+    take(1, 3)
+    share_all(1, 2, 3)
+    pair_up(1, 0)
+    add_core(1, 0, 1)
+    complete(0, 1)
+    gate(1)
+    take(1, 6)
+    share_all(1, 6)
+    project(0, 1, wout)
     go_home(0, 0)
-    project(1, 1 - c, flipped)
-    to_core(1)
     go_home(0, 1)
-    project(1, c, flipped)
-    pair_up(1)
-    for piece in range(2, 5):
+    pair_up(0, 1, (0, 2))
+    add_core(0, 1, 1)
+    complete(1, 1)
+    slopes(1)
+    project(1, 1, flipped)
+    go_home(1, 0)
+    go_home(1, 1)
+    pair_up(1, 1, (1, 2), (0, 3), (1, 3), (0, 4), (1, 4))
+    add_core(1, 1, 1)
+    for piece in (2, 3, 4):
         go_home(0, piece)
-    add_core(1, 1)
-    pick = onehot((positions, rows_all), lambda r, q: q == 4 * r + h).astype(BF)
-    own_tok[...] = mm(pick, tok[...]).astype(BF)
-    own_grad[...] = mm(pick, grad[...]).astype(BF)
-    own_disp[...] = mm(pick, disp_all[...])
-    own_comb[...] = mm(pick, comb_all[...])
-    for piece in range(5):
         go_home(1, piece)
 
     def wait_home(t):
@@ -396,13 +394,10 @@
 
     for t in range(2):
         wait_for(send.at[t, pl.ds(0, 39)], put_sem.at[t])
-        for i in range(5):
-            wait_for(rows[t].at[0, pl.ds(0, counts[i])], fwd_sem.at[t, i])
-        for i, count in enumerate(counts):
-            wait_for(rows[t].at[0, pl.ds(0, count)], cput_sem.at[t, i])
+        wait_for(rows[t].at[0, pl.ds(0, 24)], fwd_sem.at[t])
+        wait_for(rows[t].at[0], cput_sem.at[t])
         wait_for(fromcore.at[t], rput_sem.at[t])
-        for k in range(5):
-            to_pair(t, k).wait_send()
+        wait_for(frompair.at[t], zput_sem.at[t])
         wait_for(home.at[t, pl.ds(0, 63)], hput_sem.at[t])
 
 
@@ -430,8 +425,8 @@
             pltpu.VMEM((2, 64, 2, 2, width), BF),
             pltpu.VMEM((2, 64, 2, 2, width), BF),
             pltpu.VMEM((2, 64, 2, 2, width), BF),
-            pltpu.VMEM((2, 256, units), F32),
-            pltpu.VMEM((2, 256, units), BF),
+            pltpu.VMEM((2, 128, units), F32),
+            pltpu.VMEM((2, 128, units), BF),
             pltpu.VMEM((width // 128, 256, 128), F32),
             pltpu.VMEM((2, 2, 64, 2, 2, width), BF),
             pltpu.VMEM((2, 64, 2, 2, width), BF),
@@ -445,8 +440,9 @@
             pltpu.VMEM((positions * images, slots), BF),
             pltpu.VMEM((positions * images, slots), F32),
             pltpu.VMEM((2, units, width), BF),
-            dma((7,)), dma((2,)), dma((2, 6)), dma((2,)), dma((2, 5)), dma((2, 5)), dma((2, 11)), dma((2, 11)),
-            dma((2,)), dma((2, 2)), dma((2, 5)), dma((2, 5)), dma((2,)), dma((2,)), dma((2,)),
+            pltpu.VMEM((2, width, units), BF),
+            dma((7,)), dma((2,)), dma((2, 4)), dma((2,)), dma((2,)), dma((2, 3)), dma((2,)), dma((2, 2)),
+            dma((2,)), dma((2, 4)), dma((2,)), dma((2, 5)), dma((2,)), dma((2,)), dma((2,)),
         ],
         compiler_params=pltpu.CompilerParams(
             collective_id=0, has_side_effects=True, vmem_limit_bytes=58 * 1024 * 1024

time: 56.3 us -> 55 us (0.977)
  Pallas kernels: 55.5 us -> 54 us
    pallas_call x1, Pallas kernels: 55.5 us -> 54 us  [local(): pl.pallas_call(kernel, out_shape=pltpu.VMEM((positions, width), BF), in_s...]
where the time goes in v4:
time: 55 us; the launch traced here: 54.8 us
  Pallas kernels  54 us (98%)
  local copies, waits for them, and re-layouts  0.75 us (1%)
    pallas_call x1, Pallas kernels, local(): pl.pallas_call(kernel, out_shape=pltpu.VMEM((positions, width), BF), in_s...  54 us

profile of v4, /device:TPU:1, one launch (start us, length us, event | category | flops | bytes accessed | tf_op | source)
XLA Modules:
  0.0 54.8 jit_solution(13853416607821284598)
XLA Ops:
  0.0 54.0 %moe_input_grad.1 = bf16[196,1024]{1,0:T(8,128)(2,1)S(1)} custom-call(bf16[196,4,1024]{2,1,0:T(4,128)(2,1)} %bitcast.4, bf16[196,4,1024]{2,1,0:T(4,128)(2,1)} %bitcast.5, bf16[1024,128]{1,0:T(8,128)(2,1)} %keys_h.1, bf16[2,1024,1024]{2,1,0:T(8,128)(2,1)} %win_h.1, f32[2,1024]{1,0:T(2,128)} %bin_h.1, bf16[2,1024,1024]{2,1,0:T(8,128)(2,1)} %wout_h.1, ...), custom_call_target="tpu_custom_call" | custom-call | tf_op jit(solution)/shard_map/moe_input_grad/pallas_call | solution.py:410
  54.0 0.8 %copy.9 = bf16[1,196,1024]{2,1,0:T(8,128)(2,1)} copy(bf16[1,196,1024]{2,1,0:T(8,128)(2,1)S(1)} %bitcast.3) | data formatting | bytes 802816

commit v5 on v4

--- a/solution.py
+++ b/solution.py
@@ -227,10 +227,6 @@
             src_ref=part.at[t, c, s, j], dst_ref=frompair.at[t, ls, lj], send_sem=zput_sem.at[t],
             recv_sem=zgot_sem.at[t, k], device_id=pair, device_id_type=MESH,
         )
-
-    def queue(*pieces):
-        for t, k in pieces:
-            to_pair(t, k).start()
 
     def pair_up(t, u, *more):
         add_core(t, u, 0)
@@ -343,11 +339,11 @@
     share_all(1, 5)
     take(0, 3)
     share_all(0, 2, 3)
+    take(1, 2)
     pair_up(0, 0)
     add_core(0, 0, 1)
     complete(1, 0)
     slopes(0)
-    take(1, 2)
     project(1, 0, flipped)
     take(0, 6)
     share_all(0, 6)
@@ -361,15 +357,15 @@
     share_all(1, 6)
     project(0, 1, wout)
     go_home(0, 0)
+    pair_up(0, 1, (0, 2))
     go_home(0, 1)
-    pair_up(0, 1, (0, 2))
     add_core(0, 1, 1)
     complete(1, 1)
     slopes(1)
     project(1, 1, flipped)
     go_home(1, 0)
+    pair_up(1, 1, (1, 2), (0, 3), (1, 3), (0, 4), (1, 4))
     go_home(1, 1)
-    pair_up(1, 1, (1, 2), (0, 3), (1, 3), (0, 4), (1, 4))
     add_core(1, 1, 1)
     for piece in (2, 3, 4):
         go_home(0, piece)

time: 55 us -> 54.1 us (0.984)
  Pallas kernels: 54 us -> 53.3 us
    pallas_call x1, Pallas kernels: 54 us -> 53.3 us  [local(): pl.pallas_call(kernel, out_shape=pltpu.VMEM((positions, width), BF), in_s...]
where the time goes in v5:
time: 54.1 us; the launch traced here: 54 us
  Pallas kernels  53.3 us (99%)
  local copies, waits for them, and re-layouts  0.75 us (1%)
    pallas_call x1, Pallas kernels, local(): pl.pallas_call(kernel, out_shape=pltpu.VMEM((positions, width), BF), in_s...  53.3 us

profile of v5, /device:TPU:1, one launch (start us, length us, event | category | flops | bytes accessed | tf_op | source)
XLA Modules:
  0.0 54.0 jit_solution(7821812511260713932)
XLA Ops:
  0.0 53.3 %moe_input_grad.1 = bf16[196,1024]{1,0:T(8,128)(2,1)S(1)} custom-call(bf16[196,4,1024]{2,1,0:T(4,128)(2,1)} %bitcast.4, bf16[196,4,1024]{2,1,0:T(4,128)(2,1)} %bitcast.5, bf16[1024,128]{1,0:T(8,128)(2,1)} %keys_h.1, bf16[2,1024,1024]{2,1,0:T(8,128)(2,1)} %win_h.1, f32[2,1024]{1,0:T(2,128)} %bin_h.1, bf16[2,1024,1024]{2,1,0:T(8,128)(2,1)} %wout_h.1, ...), custom_call_target="tpu_custom_call" | custom-call | tf_op jit(solution)/shard_map/moe_input_grad/pallas_call | solution.py:406
  53.3 0.8 %copy.9 = bf16[1,196,1024]{2,1,0:T(8,128)(2,1)} copy(bf16[1,196,1024]{2,1,0:T(8,128)(2,1)S(1)} %bitcast.3) | data formatting | bytes 802816
